TPU v7x, 32 devices: a whole 2x2x4 slice. The times are simulated.
32 devices in a mesh: group: 4 (over y, x), patch: 8 (over z, core).
Axes of the slice: x: 2, y: 2, z: 4, core: 2. Of those that a mesh axis runs over, the one named last changes fastest.
Arguments:
- node_tape: bfloat16 [4, 8192, 512], P('group', 'patch'), may hold values from -6 to 6
- edge_tape: bfloat16 [4, 8192, 512], P('group', 'patch'), may hold values from -6 to 6
- node_cot: bfloat16 [4, 8192, 512], P('group', 'patch'), may hold values from -6 to 6
- edge_cot: bfloat16 [4, 8192, 512], P('group', 'patch'), may hold values from -6 to 6
- w_edge_in: bfloat16 [1536, 512], replicated, may hold values from -0.15625 to 0.15625
- w_edge_out: bfloat16 [512, 512], replicated, may hold values from -0.25 to 0.25
- gain_edge: float32 [512], replicated, may hold values from 0.1 to 1.9
- w_node_in: bfloat16 [1024, 512], replicated, may hold values from -0.1875 to 0.1875
- w_node_out: bfloat16 [512, 512], replicated, may hold values from -0.25 to 0.25
- gain_node: float32 [512], replicated, may hold values from 0.1 to 1.9
- senders: int32 [64, 128], P('patch'), may hold values from 0 to 1279
- receivers: int32 [64, 128], P('patch'), may hold values from 0 to 1023
- tile_count: int32 [8], P('patch'), may hold values from 1 to 8, as said below
- send_rows: int32 [8, 256], P('patch'), may hold values from 0 to 1023
Outputs:
- edge_grad: bfloat16 [4, 8192, 512], P('group', 'patch')
- node_grad: bfloat16 [4, 8192, 512], P('group', 'patch')
- grad_edge_in: float32 [1536, 512], P('patch')
- grad_edge_out: float32 [512, 512], P('patch')
- grad_gain_edge: float32 [512], P('patch')
- grad_node_in: float32 [1024, 512], P('patch')
- grad_node_out: float32 [512, 512], P('patch')
- grad_gain_node: float32 [512], P('patch')
Inputs may be any that keep to these rules, and one draw needn't show every extreme that they name: Tiles 0 to tile_count - 1 of a patch's 8 slots hold edges, the rest are padding; some patch has all 8 live. `senders`: A value s below 1024 is a node of the edge's own patch; 1024 + k is the k-th halo row that patch receives, rows p * 32 to (p + 1) * 32 - 1 coming from patch p. `receivers`: A node of the edge's own patch. `send_rows`: entry p * 32 + j of patch q's list is the own node whose latent is the j-th halo row patch p receives from q; every patch sends exactly 32 rows to every patch.
All inputs are finite; a program needn't handle non-finite values.
Results may differ from a plain program's by a relative error of at most 0.014.
Values may be sent and summed in bfloat16 or wider, within the bound.
A program may use at most 128 MiB of HBM per device.

v0:
```python
import functools

import jax
import jax.numpy as jnp
from jax import lax
from jax.experimental import pallas as pl
from jax.experimental.pallas import tpu as pltpu
from jax.sharding import PartitionSpec as P

epsilon = 1e-05
BF = jnp.bfloat16
F32 = jnp.float32
LANES = 128
PACK = 16
MESH = pl.DeviceIdType.MESH


def dot(left, right):
    return jnp.dot(left, right, preferred_element_type=F32)


def dot_rt(left, right):
    return lax.dot_general(left, right, (((1,), (1,)), ((), ())), preferred_element_type=F32)


def dot_lt(left, right):
    return lax.dot_general(left, right, (((0,), (0,)), ((), ())), preferred_element_type=F32)


def sigmoid(values):
    return 1.0 / (1.0 + jnp.exp(-values))


def silu_slope(values):
    squash = sigmoid(values)
    return squash * (1.0 + values * (1.0 - squash))


def normalize(values):
    centred = values - jnp.mean(values, axis=1, keepdims=True)
    inverse = lax.rsqrt(jnp.mean(centred * centred, axis=1, keepdims=True) + epsilon)
    return (centred * inverse, inverse)


def normalize_back(upstream, normed, inverse):
    return inverse * (
        upstream
        - jnp.mean(upstream, axis=1, keepdims=True)
        - normed * jnp.mean(upstream * normed, axis=1, keepdims=True)
    )


def hot(index, shape, axis, base):
    return jnp.where(lax.broadcasted_iota(jnp.int32, shape, axis) + base == index, 1.0, 0.0).astype(
        BF
    )


class Copies:
    def __init__(self, send_sems, recv_sems):
        self.send_sems, self.recv_sems, self.used = send_sems, recv_sems, 0

    def start(self, source, target, device):
        copy = pltpu.make_async_remote_copy(
            src_ref=source,
            dst_ref=target,
            send_sem=self.send_sems.at[self.used],
            recv_sem=self.recv_sems.at[self.used],
            device_id=device,
            device_id_type=MESH,
        )
        self.used += 1
        copy.start()
        return copy


def wait_all(copies):
    for copy in copies:
        copy.wait()


class Reduction:
    def __init__(self, copies, refs, depth, middle, place):
        self.copies, self.depth, self.middle = copies, depth, middle
        self.g, self.rc, self.a, self.r1x, self.r1y, self.b0, self.b1 = refs[:7]
        self.r2x, self.r2y, self.c, self.r3, self.f = refs[7:]
        self.gi, self.p, self.core, self.z, self.gx, self.gy, self.zs = place
        self.xpeer = {"group": self.gi + 1 - 2 * self.gx, "patch": self.p}
        self.ypeer = {"group": self.gi + 2 - 4 * self.gy, "patch": self.p}
        self.low = pl.ds(0, middle)
        self.high = pl.ds(middle, depth - middle)

    def step0(self):
        other = {"group": self.gi, "patch": self.p + 1 - 2 * self.core}
        self.wait = [self.copies.start(self.g.at[1 - self.core], self.rc, other)]

    def step1(self):
        wait_all(self.wait)

        @pl.loop(0, self.zs)
        def _(k):
            self.a[k] = (self.g[self.core, k].astype(F32) + self.rc[k].astype(F32)).astype(BF)

        self.wait = [
            self.copies.start(self.a.at[:, 1 - self.gx, :, self.low], self.r1x, self.xpeer),
            self.copies.start(self.a.at[:, :, 1 - self.gy, self.high], self.r1y, self.ypeer),
        ]

    def step2(self):
        wait_all(self.wait)

        @pl.loop(0, self.zs)
        def _(k):
            self.b0[k] = (
                self.a[k, self.gx, :, self.low].astype(F32) + self.r1x[k].astype(F32)
            ).astype(BF)
            self.b1[k] = (
                self.a[k, :, self.gy, self.high].astype(F32) + self.r1y[k].astype(F32)
            ).astype(BF)

        self.wait = [
            self.copies.start(self.b0.at[:, 1 - self.gy], self.r2y, self.ypeer),
            self.copies.start(self.b1.at[:, 1 - self.gx], self.r2x, self.xpeer),
        ]

    def step3(self):
        wait_all(self.wait)

        @pl.loop(0, self.zs)
        def _(k):
            self.c[k, self.low] = (
                self.b0[k, self.gy].astype(F32) + self.r2y[k].astype(F32)
            ).astype(BF)
            self.c[k, self.high] = (
                self.b1[k, self.gx].astype(F32) + self.r2x[k].astype(F32)
            ).astype(BF)

        self.wait = []
        for step in range(1, self.zs):
            there = lax.rem(self.z + step, self.zs)
            self.wait.append(
                self.copies.start(
                    self.c.at[there],
                    self.r3.at[step - 1],
                    {"group": self.gi, "patch": there * 2 + self.core},
                )
            )

    def step4(self):
        wait_all(self.wait)
        total = self.c[self.z].astype(F32)
        for step in range(1, self.zs):
            total += self.r3[step - 1].astype(F32)
        self.f[self.gx, self.gy] = total.astype(BF)
        low = self.f.at[self.gx, self.gy, self.low]
        high = self.f.at[self.gx, self.gy, self.high]
        self.wait = [
            self.copies.start(low, low, self.ypeer),
            self.copies.start(high, high, self.xpeer),
        ]

    def step5(self):
        wait_all(self.wait)
        low = self.f.at[self.gx, :, self.low]
        high = self.f.at[:, self.gy, self.high]
        self.wait = [
            self.copies.start(low, low, self.xpeer),
            self.copies.start(high, high, self.ypeer),
        ]

    def step6(self, outs, factor):
        wait_all(self.wait)
        for quarter in range(4):
            row = 0
            for out in outs:
                size = out.shape[0]
                out[:, quarter * LANES : (quarter + 1) * LANES] = (
                    self.f[quarter // 2, quarter % 2, row : row + size].astype(F32) * factor
                )
                row += size


def kernel(sizes, *refs):
    n_group, n_patch, padded, tile, tile_edges, fused, factor = sizes
    stored = refs[:8]
    gain_e, gain_n, send_tiles, recv_tiles, list_tiles, count = refs[8:14]
    edge_out, node_out, o_ei, o_eo, o_ni, o_no, o_gain = refs[14:21]
    loaded = refs[21:29]
    node, edge, w_ei, w_eo, w_ni, w_no, node_cot, edge_cot = loaded
    edge_grad, node_grad, load_sems, store_sems = refs[29:33]
    send_col, send_row, recv_col, recv_row, list_col, list_row = refs[33:39]
    refs = refs[15:]
    (
        outgoing,
        incoming,
        spread,
        returned,
        x_s,
        x_r,
        e_first,
        hidden,
        normed,
        inverse,
        message,
        joined,
        n_hidden,
        g_second,
        g_first,
        acc,
        gj,
        ge_second,
        ge_first,
        gs,
        gr,
        gains,
        send_sems,
        recv_sems,
    ) = refs[24:48]
    nodes, width = node.shape
    edges = edge.shape[0]
    halo = n_patch * padded
    gi = lax.axis_index("group")
    p = lax.axis_index("patch")
    core = lax.rem(p, 2)
    z = lax.div(p, 2)
    gx = lax.rem(gi, 2)
    gy = lax.div(gi, 2)
    copies = Copies(send_sems, recv_sems)
    loads = [
        pltpu.make_async_copy(source, target, load_sems.at[order])
        for order, (source, target) in enumerate(zip(stored, loaded))
    ]
    for load in loads:
        load.start()

    barrier = pltpu.get_barrier_semaphore()
    peers = [{"group": gi, "patch": lax.rem(p + d, n_patch)} for d in range(1, n_patch)]
    greeted = list(peers)
    if fused:
        greeted.append({"group": gi + 1 - 2 * gx, "patch": p})
        greeted.append({"group": gi + 2 - 4 * gy, "patch": p})
    for peer in greeted:
        pl.semaphore_signal(barrier, inc=1, device_id=peer, device_id_type=MESH)

    for tiles, column, line in (
        (list_tiles, list_col, list_row),
        (send_tiles, send_col, send_row),
        (recv_tiles, recv_col, recv_row),
    ):
        turned = jnp.transpose(tiles[...].astype(F32)).astype(jnp.int32)
        for order in range(line.shape[1] // LANES):
            span = slice(order * LANES, (order + 1) * LANES)
            column[span, :] = turned[:, order : order + 1]
            line[:, span] = tiles[order : order + 1, :]

    loads[0].wait()
    chosen = dot(hot(list_col[...], (halo, nodes), 1, 0), node[...]).astype(BF)
    outgoing[...] = chosen.reshape(n_patch, padded, width)
    pl.semaphore_wait(barrier, len(greeted))
    moving = [
        copies.start(outgoing.at[lax.rem(p + d, n_patch)], incoming.at[p], peers[d - 1])
        for d in range(1, n_patch)
    ]
    incoming[p] = outgoing[p]
    gains[...] = jnp.zeros_like(gains)

    loads[1].wait()
    loads[2].wait()

    def rows_of(k):
        return pl.ds(pl.multiple_of(k * tile, tile), tile)

    @pl.loop(0, edges // tile)
    def _(k):
        rows = rows_of(k)
        latent = dot(hot(recv_col[rows, :], (tile, nodes), 1, 0), node[...]).astype(BF)
        x_r[rows, :] = latent
        e_first[rows, :] = dot(edge[rows, :], w_ei[:width, :]) + dot(latent, w_ei[2 * width :, :])

    loads[3].wait()
    wait_all(moving)

    def live_of(k):
        slot = lax.broadcasted_iota(jnp.int32, (tile, 1), 0) + k * tile
        return jnp.where(slot < count[0] * tile_edges, 1.0, 0.0)

    @pl.loop(0, edges // tile)
    def _(k):
        rows = rows_of(k)
        index = send_col[rows, :]
        latent = dot(hot(index, (tile, nodes), 1, 0), node[...])
        latent += dot(hot(index, (tile, halo), 1, nodes), incoming[...].reshape(halo, width))
        latent = latent.astype(BF)
        x_s[rows, :] = latent
        first = e_first[rows, :] + dot(latent, w_ei[width : 2 * width, :])
        e_first[rows, :] = first
        hid = (first * sigmoid(first)).astype(BF)
        hidden[rows, :] = hid
        norm, inv = normalize(dot(hid, w_eo[...]))
        normed[rows, :] = norm
        inverse[rows, :] = inv
        message[rows, :] = (live_of(k) * (gain_e[...] * norm)).astype(BF)

    for load in loads[4:]:
        load.wait()

    @pl.loop(0, nodes // tile)
    def _(k):
        rows = rows_of(k)
        got = dot(hot(recv_row[...], (tile, edges), 0, k * tile), message[...]).astype(BF)
        joined[rows, :] = got
        first = dot(node[rows, :], w_ni[:width, :]) + dot(got, w_ni[width:, :])
        hid = (first * sigmoid(first)).astype(BF)
        n_hidden[rows, :] = hid
        norm, inv = normalize(dot(hid, w_no[...]))
        up = node_cot[rows, :].astype(F32)
        gains[1:2, :] += jnp.sum(up * norm, axis=0, keepdims=True)
        second = normalize_back(up * gain_n[...], norm, inv).astype(BF)
        g_second[rows, :] = second
        grad = (dot_rt(second, w_no[...]) * silu_slope(first)).astype(BF)
        g_first[rows, :] = grad
        acc[rows, :] = up + dot_rt(grad, w_ni[:width, :])
        gj[rows, :] = dot_rt(grad, w_ni[width:, :]).astype(BF)

    if fused:
        red_n_refs, red_e_refs, red_o_refs = refs[48:60], refs[60:72], refs[72:84]
        zs = n_patch // 2
        place = (gi, p, core, z, gx, gy, zs)
        g_n, g_e, g_o = red_n_refs[0], red_e_refs[0], red_o_refs[0]
        red_n = Reduction(copies, red_n_refs, g_n.shape[-2], red_n_refs[3].shape[-2], place)
        red_e = Reduction(copies, red_e_refs, g_e.shape[-2], red_e_refs[3].shape[-2], place)
        red_o = Reduction(copies, red_o_refs, g_o.shape[-2], red_o_refs[3].shape[-2], place)

        def put(target, k, row, size, value):
            value = value.astype(BF)
            for c in range(2):
                for quarter in range(4):
                    target[c, k, quarter // 2, quarter % 2, row : row + size, :] = value[
                        c * size : (c + 1) * size, quarter * LANES : (quarter + 1) * LANES
                    ]

        def terms(target, k, row, size, left, right, first=0):
            span = pl.ds(pl.multiple_of(k * 2 * size, LANES), 2 * size)
            put(target, k + first, row, size, dot_lt(left[:, span], right))

        d_ni, d_no = o_ni.shape[0], o_no.shape[0]
        d_ei, d_eo = o_ei.shape[0], o_eo.shape[0]
        half = zs // 2

        @pl.loop(0, half)
        def _(k):
            terms(g_n, k, 0, d_ni, node, g_first[...])
            terms(g_n, k, 0, d_ni, joined, g_first[...], half)

        @pl.loop(0, zs)
        def _(k):
            terms(g_n, k, d_ni, d_no, n_hidden, g_second[...])

        red_n.step0()
    else:
        o_ni[:width, :] = dot_lt(node[...], g_first[...])
        o_ni[width:, :] = dot_lt(joined[...], g_first[...])
        o_no[...] = dot_lt(n_hidden[...], g_second[...])

    def edge_back(k):
        rows = rows_of(k)
        taken = dot(hot(recv_col[rows, :], (tile, nodes), 1, 0), gj[...])
        live = live_of(k)
        norm = normed[rows, :]
        grad = live * (edge_cot[rows, :].astype(F32) + taken)
        gains[0:1, :] += jnp.sum(grad * norm, axis=0, keepdims=True)
        second = normalize_back(grad * gain_e[...], norm, inverse[rows, :]).astype(BF)
        ge_second[rows, :] = second
        ge_first[rows, :] = (
            dot_rt(second, w_eo[...]) * silu_slope(e_first[rows, :])
        ).astype(BF)

    count_tiles = edges // tile
    pl.loop(0, count_tiles)(edge_back)

    if fused:
        red_n.step1()
        blocks = 2 * d_ei
        for k in range(zs):
            start, stop = k * blocks, (k + 1) * blocks
            parts = []
            for order, source in enumerate((edge, x_s, x_r)):
                lo = max(start, order * width) - order * width
                hi = min(stop, (order + 1) * width) - order * width
                if lo < hi:
                    parts.append(dot_lt(source[:, lo:hi], ge_first[...]))
            value = parts[0] if len(parts) == 1 else jnp.concatenate(parts, axis=0)
            put(g_e, k, 0, d_ei, value)

        red_e.step0()
        red_n.step2()

        @pl.loop(0, zs)
        def _(k):
            terms(g_o, k, 0, d_eo, hidden, ge_second[...])
            total = gains[...]
            put(g_o, k, d_eo, PACK, jnp.concatenate([total, total], axis=0))

        red_o.step0()
    else:
        o_ei[:width, :] = dot_lt(edge[...], ge_first[...])
        o_ei[width : 2 * width, :] = dot_lt(x_s[...], ge_first[...])
        o_ei[2 * width :, :] = dot_lt(x_r[...], ge_first[...])
        o_eo[...] = dot_lt(hidden[...], ge_second[...])
        o_gain[...] = gains[...]

    def input_back(k):
        rows = rows_of(k)
        grad = ge_first[rows, :]
        gs[rows, :] = dot_rt(grad, w_ei[width : 2 * width, :]).astype(BF)
        gr[rows, :] = dot_rt(grad, w_ei[2 * width :, :]).astype(BF)

    pl.loop(0, count_tiles)(input_back)
    sums = dot(hot(send_row[...], (halo, edges), 0, nodes), gs[...]).astype(BF)
    spread[...] = sums.reshape(n_patch, padded, width)
    moving = [
        copies.start(spread.at[lax.rem(p + d, n_patch)], returned.at[p], peers[d - 1])
        for d in range(1, n_patch)
    ]
    returned[p] = spread[p]
    if fused:
        red_e.step1()
        red_n.step3()

    @pl.loop(0, count_tiles)
    def _(k):
        rows = rows_of(k)
        edge_grad[rows, :] = (
            live_of(k) * edge_cot[rows, :].astype(F32) + dot_rt(ge_first[rows, :], w_ei[:width, :])
        ).astype(BF)

    stores = [pltpu.make_async_copy(edge_grad, edge_out, store_sems.at[0])]
    stores[0].start()
    if fused:
        red_o.step1()
        red_n.step4()

    def gather_back(k):
        rows = rows_of(k)
        acc[rows, :] += dot(hot(send_row[...], (tile, edges), 0, k * tile), gs[...]) + dot(
            hot(recv_row[...], (tile, edges), 0, k * tile), gr[...]
        )

    middle = nodes // tile // 2
    pl.loop(0, middle)(gather_back)
    if fused:
        red_e.step2()
        red_o.step2()
        red_n.step5()
    pl.loop(middle, nodes // tile)(gather_back)
    if fused:
        red_e.step3()
        red_o.step3()
        red_n.step6((o_ni, o_no), factor)
    wait_all(moving)

    @pl.loop(0, nodes // tile)
    def _(k):
        rows = rows_of(k)
        node_grad[rows, :] = (
            acc[rows, :]
            + dot(
                hot(list_row[...], (tile, halo), 0, k * tile),
                returned[...].reshape(halo, width),
            )
        ).astype(BF)

    stores.append(pltpu.make_async_copy(node_grad, node_out, store_sems.at[1]))
    stores[1].start()
    if fused:
        red_e.step4()
        red_o.step4()
        red_e.step5()
        red_o.step5()
        red_e.step6((o_ei,), factor)
        red_o.step6((o_eo,), factor)
        piece = o_gain.shape[1]
        own = jnp.zeros(o_gain.shape, F32)
        for quarter in range(4):
            lane = lax.broadcasted_iota(jnp.int32, (LANES, piece), 0) + quarter * LANES
            want = lax.broadcasted_iota(jnp.int32, (LANES, piece), 1) + p * piece
            pick = jnp.where(lane == want, 1.0, 0.0).astype(BF)
            own += dot(red_o.f[quarter // 2, quarter % 2, d_eo : d_eo + PACK], pick)
        o_gain[...] = own * factor
    for store in stores:
        store.wait()


def reduction_scratch(zs, depth, middle):
    rest = depth - middle
    shapes = (
        (2, zs, 2, 2, depth),
        (zs, 2, 2, depth),
        (zs, 2, 2, depth),
        (zs, 2, middle),
        (zs, 2, rest),
        (zs, 2, middle),
        (zs, 2, rest),
        (zs, rest),
        (zs, middle),
        (zs, depth),
        (zs - 1, depth),
        (2, 2, depth),
    )
    return [pltpu.VMEM(shape + (LANES,), BF) for shape in shapes]


def tiles_of(index):
    rows = -(-index.shape[0] // LANES)
    full = -(-rows // 8) * 8
    return jnp.pad(index, (0, full * LANES - index.shape[0])).reshape(full, LANES)


def local(
    n_group,
    n_patch,
    node_tape,
    edge_tape,
    node_cot,
    edge_cot,
    w_edge_in,
    w_edge_out,
    gain_edge,
    w_node_in,
    w_node_out,
    gain_node,
    senders,
    receivers,
    tile_count,
    send_rows,
):
    nodes, width = node_tape.shape[1:]
    edges = edge_tape.shape[1]
    listed = send_rows.shape[1]
    peer_rows = listed // n_patch
    padded = -(-peer_rows // PACK) * PACK
    halo = n_patch * padded
    tile = min(2 * LANES, nodes, edges)
    factor = float(n_group * n_patch * edges) ** (-0.5)

    flat = senders.reshape(-1)
    beyond = flat - nodes
    if padded != peer_rows:
        beyond = beyond // peer_rows * padded + beyond % peer_rows
        flat = jnp.where(flat < nodes, flat, nodes + beyond)
    lists = jnp.pad(
        send_rows.reshape(n_patch, peer_rows), ((0, 0), (0, padded - peer_rows)), constant_values=-1
    )
    recv = receivers.reshape(-1)

    weights = (w_edge_in, w_edge_out, w_node_in, w_node_out)
    depths = [w.shape[0] // n_patch for w in weights]
    zs = n_patch // 2
    fused = (
        n_group == 4
        and n_patch % 4 == 0
        and width == 4 * LANES
        and all(d % PACK == 0 and 2 * d % LANES == 0 for d in depths)
    )
    own_rows = (node_tape[0], edge_tape[0], node_cot[0], edge_cot[0])
    operands = own_rows[:2] + weights + own_rows[2:]
    slots = -(-halo // LANES) * LANES
    scratch = [pltpu.VMEM(operand.shape, BF) for operand in operands]
    scratch += [
        pltpu.VMEM((edges, width), BF),
        pltpu.VMEM((nodes, width), BF),
        pltpu.SemaphoreType.DMA((len(operands),)),
        pltpu.SemaphoreType.DMA((2,)),
    ]
    for length in (edges, edges, slots):
        scratch += [pltpu.VMEM((length, 1), jnp.int32), pltpu.VMEM((1, length), jnp.int32)]
    scratch += [
        pltpu.VMEM((n_patch, padded, width), BF),
        pltpu.VMEM((n_patch, padded, width), BF),
        pltpu.VMEM((n_patch, padded, width), BF),
        pltpu.VMEM((n_patch, padded, width), BF),
        pltpu.VMEM((edges, width), BF),
        pltpu.VMEM((edges, width), BF),
        pltpu.VMEM((edges, width), F32),
        pltpu.VMEM((edges, width), BF),
        pltpu.VMEM((edges, width), F32),
        pltpu.VMEM((edges, 1), F32),
        pltpu.VMEM((edges, width), BF),
        pltpu.VMEM((nodes, width), BF),
        pltpu.VMEM((nodes, width), BF),
        pltpu.VMEM((nodes, width), BF),
        pltpu.VMEM((nodes, width), BF),
        pltpu.VMEM((nodes, width), F32),
        pltpu.VMEM((nodes, width), BF),
        pltpu.VMEM((edges, width), BF),
        pltpu.VMEM((edges, width), BF),
        pltpu.VMEM((edges, width), BF),
        pltpu.VMEM((edges, width), BF),
        pltpu.VMEM((PACK, width), F32),
    ]
    n_copies = 2 * (n_patch - 1)
    if fused:
        d_ei, d_eo, d_ni, d_no = depths
        depth_n = d_ni + d_no
        depth_o = d_eo + PACK
        piece = width // n_patch
        scratch_n = reduction_scratch(zs, depth_n, depth_n // 2 // PACK * PACK)
        scratch_e = reduction_scratch(zs, d_ei, d_ei // 2 // PACK * PACK)
        scratch_e += reduction_scratch(zs, depth_o, depth_o // 2 // PACK * PACK)
        n_copies += 3 * (9 + zs - 1)
    else:
        d_ei, d_eo, d_ni, d_no = [w.shape[0] for w in weights]
        scratch_n, scratch_e = [], []
        piece = width
    scratch += [pltpu.SemaphoreType.DMA((n_copies,)), pltpu.SemaphoreType.DMA((n_copies,))]
    scratch += scratch_n + scratch_e

    vmem = pl.BlockSpec(memory_space=pltpu.VMEM)
    anywhere = pl.BlockSpec(memory_space=pl.ANY)
    sizes = (n_group, n_patch, padded, tile, senders.shape[1], fused, factor)
    edge_grad, node_grad, p_ei, p_eo, p_ni, p_no, p_gain = pl.pallas_call(
        functools.partial(kernel, sizes),
        out_shape=[
            jax.ShapeDtypeStruct((edges, width), BF),
            jax.ShapeDtypeStruct((nodes, width), BF),
            jax.ShapeDtypeStruct((d_ei, width), F32),
            jax.ShapeDtypeStruct((d_eo, width), F32),
            jax.ShapeDtypeStruct((d_ni, width), F32),
            jax.ShapeDtypeStruct((d_no, width), F32),
            jax.ShapeDtypeStruct((PACK, piece), F32),
        ],
        in_specs=[anywhere] * 8 + [vmem] * 5 + [pl.BlockSpec(memory_space=pltpu.SMEM)],
        out_specs=[anywhere] * 2 + [vmem] * 5,
        scratch_shapes=scratch,
        compiler_params=pltpu.CompilerParams(
            collective_id=0, has_side_effects=True, vmem_limit_bytes=63 * 1024 * 1024
        ),
    )(
        *operands,
        gain_edge[None],
        gain_node[None],
        tiles_of(flat),
        tiles_of(recv),
        tiles_of(lists.reshape(-1)),
        tile_count,
    )
    if fused:
        return (edge_grad[None], node_grad[None], p_ei, p_eo, p_gain[0], p_ni, p_no, p_gain[1])

    def summed(value):
        part = lax.psum_scatter(value, "patch", scatter_dimension=0, tiled=True)
        return lax.psum(part.astype(BF), "group").astype(F32) * factor

    return (
        edge_grad[None],
        node_grad[None],
        summed(p_ei),
        summed(p_eo),
        summed(p_gain[0]),
        summed(p_ni),
        summed(p_no),
        summed(p_gain[1]),
    )


def solution(mesh):
    member = P("group", "patch", None)
    placed = (member,) * 4 + (P(),) * 6
    placed += (P("patch", None), P("patch", None), P("patch"), P("patch", None))
    rows = P("patch", None)
    return jax.shard_map(
        functools.partial(local, mesh.shape["group"], mesh.shape["patch"]),
        mesh=mesh,
        in_specs=placed,
        out_specs=(member, member, rows, rows, P("patch"), rows, rows, P("patch")),
        check_vma=False,
    )
```

profile of v0, /device:TPU:0, one launch (start us, length us, event | category | flops | bytes accessed | tf_op | source)
XLA Modules:
  0.0 83.6 jit_solution(13014725849271418350)
XLA Ops:
  0.6 1.3 %pad_bitcast_fusion.refs_12_ = s32[8,128]{1,0:T(8,128)} fusion(s32[256]{0:T(256)} %bitcast.23), kind=kLoop, calls=%fused_computation | loop fusion | bytes 5120 | tf_op jit(solution)/shard_map/reshape | solution.py:516
  2.6 73.7 %shard_map.197 = (bf16[1024,512]{1,0:T(8,128)(2,1)}, bf16[1024,512]{1,0:T(8,128)(2,1)}, f32[192,512]{1,0:T(8,128)}, f32[64,512]{1,0:T(8,128)}, f32[128,512]{1,0:...) custom-call(bf16[1024,512]{1,0:T(8,128)(2,1)} %bitcast.15, bf16[1024,512]{1,0:T(8,128)(2,1)} %bitcast.16, ...), custom_call_target="tpu_custom_call" | custom-call | tf_op jit(solution)/shard_map/pallas_call | solution.py:621
  76.2 0.0 copy-start
  76.2 1.3 %slice_bitcast_fusion = (f32[64]{0:T(128)}, f32[64]{0:T(128)}) fusion(f32[16,64]{1,0:T(8,128)} %get-tuple-element.19), kind=kLoop, calls=%fused_computation.1 | loop fusion | bytes 1024 | tf_op jit(solution)/shard_map/squeeze | solution.py:648
  77.5 0.0 copy-start.1
  77.5 2.3 %copy.29 = bf16[1,1024,512]{2,1,0:T(8,128)(2,1)} copy(bf16[1,1024,512]{2,1,0:T(8,128)(2,1)} %bitcast.20) | data formatting | bytes 2097152
  79.8 0.0 copy-done
  79.9 0.0 copy-start.4
  79.9 0.0 copy-start.2
  79.9 0.0 copy-start.3
  79.9 1.0 %copy.30 = bf16[1,1024,512]{2,1,0:T(8,128)(2,1)} copy(bf16[1,1024,512]{2,1,0:T(8,128)(2,1)S(1)} %bitcast.19) | data formatting | bytes 2097152
  80.8 0.0 copy-done.1
  80.8 0.7 copy.31
  81.6 0.0 copy-done.4
  81.6 0.7 copy.32
  82.2 0.0 copy-done.2
  82.2 0.7 copy.33
  82.9 0.0 copy-done.3
  82.9 0.7 copy.34
Async XLA Ops:
  76.2 3.6 %copy-start = (bf16[1024,512]{1,0:T(8,128)(2,1)S(1)}, bf16[1024,512]{1,0:T(8,128)(2,1)}, u32[]{:S(2)}) copy-start(bf16[1024,512]{1,0:T(8,128)(2,1)} %get-tuple-element.16) | copy-start | bytes 3145732
  77.5 3.3 %copy-start.1 = (f32[192,512]{1,0:T(8,128)S(1)}, f32[192,512]{1,0:T(8,128)}, u32[]{:S(2)}) copy-start(f32[192,512]{1,0:T(8,128)} %get-tuple-element.34) | copy-start | bytes 1179652
  79.9 1.7 %copy-start.4 = (f32[64,512]{1,0:T(8,128)S(1)}, f32[64,512]{1,0:T(8,128)}, u32[]{:S(2)}) copy-start(f32[64,512]{1,0:T(8,128)} %get-tuple-element.35) | copy-start | bytes 393220
  79.9 2.4 %copy-start.2 = (f32[128,512]{1,0:T(8,128)S(1)}, f32[128,512]{1,0:T(8,128)}, u32[]{:S(2)}) copy-start(f32[128,512]{1,0:T(8,128)} %get-tuple-element.37) | copy-start | bytes 786436
  79.9 3.1 %copy-start.3 = (f32[64,512]{1,0:T(8,128)S(1)}, f32[64,512]{1,0:T(8,128)}, u32[]{:S(2)}) copy-start(f32[64,512]{1,0:T(8,128)} %get-tuple-element.38) | copy-start | bytes 393220
where the time goes:
time: 83.9 us; the launch traced here: 83.6 us
  Pallas kernels  73.7 us (88%)
  local copies, waits for them, and re-layouts  8.62 us (10%)
  between operations  1.31 us (2%)
    pallas_call x1, Pallas kernels, local(): pl.pallas_call(functools.partial(kernel, sizes), out_shape=[jax.ShapeDtyp...  73.7 us
    unnamed x16, local copies, waits for them, and re-layouts  6.06 us

commit v1 on v0

v1 whole, which is shorter than its diff:
```python
import functools

import jax
import jax.numpy as jnp
from jax import lax
from jax.experimental import pallas as pl
from jax.experimental.pallas import tpu as pltpu
from jax.sharding import PartitionSpec as P

epsilon = 1e-05
BF = jnp.bfloat16
F32 = jnp.float32
LANES = 128
PACK = 16
MESH = pl.DeviceIdType.MESH


def dot(left, right):
    return jnp.dot(left, right, preferred_element_type=F32)


def dot_rt(left, right):
    return lax.dot_general(left, right, (((1,), (1,)), ((), ())), preferred_element_type=F32)


def dot_lt(left, right):
    return lax.dot_general(left, right, (((0,), (0,)), ((), ())), preferred_element_type=F32)


def silu_pair(values):
    squash = 0.5 * jnp.tanh(0.5 * values) + 0.5
    active = values * squash
    return (active, squash + active * (1.0 - squash))


def normalize(values):
    centred = values - jnp.mean(values, axis=1, keepdims=True)
    inverse = lax.rsqrt(jnp.mean(centred * centred, axis=1, keepdims=True) + epsilon)
    return (centred * inverse, inverse)


def normalize_back(upstream, normed, inverse):
    return inverse * (
        upstream
        - jnp.mean(upstream, axis=1, keepdims=True)
        - normed * jnp.mean(upstream * normed, axis=1, keepdims=True)
    )


def hot(index, shape, axis, base):
    return jnp.where(lax.broadcasted_iota(jnp.int32, shape, axis) + base == index, 1.0, 0.0).astype(
        BF
    )


class Copies:
    def __init__(self, send_sems, recv_sems):
        self.send_sems, self.recv_sems, self.used = send_sems, recv_sems, 0

    def start(self, source, target, device):
        copy = pltpu.make_async_remote_copy(
            src_ref=source,
            dst_ref=target,
            send_sem=self.send_sems.at[self.used],
            recv_sem=self.recv_sems.at[self.used],
            device_id=device,
            device_id_type=MESH,
        )
        self.used += 1
        copy.start()
        return copy


def wait_all(copies):
    for copy in copies:
        copy.wait()


class Place:
    def __init__(self, n_patch):
        self.gi = lax.axis_index("group")
        self.p = lax.axis_index("patch")
        self.core = lax.rem(self.p, 2)
        self.z = lax.div(self.p, 2)
        self.zs = n_patch // 2
        self.partner = {"group": self.gi, "patch": self.p + 1 - 2 * self.core}
        gx, gy = lax.rem(self.gi, 2), lax.div(self.gi, 2)
        flip_x, flip_y = 1 - 2 * gx, 2 - 4 * gy
        self.members = [self.gi + flip_x, self.gi + flip_y, self.gi + flip_x + flip_y]

    def member(self, order):
        return {"group": self.members[order], "patch": self.p}


class Reduction:
    def __init__(self, copies, refs, place):
        self.copies, self.place = copies, place
        self.g, self.rc, self.a, self.rx, self.c, self.r3, self.f = refs
        self.pairs, self.moves = [], []

    def put(self, k, row, size, value):
        value = value.astype(BF)
        for c in range(2):
            for quarter in range(4):
                self.g[c, k, quarter, row : row + size, :] = value[
                    c * size : (c + 1) * size, quarter * LANES : (quarter + 1) * LANES
                ]

    def pair(self, k):
        here = self.place
        self.pairs.append(
            self.copies.start(self.g.at[1 - here.core, k], self.rc.at[k], here.partner)
        )

    def spread(self, first, last):
        here = self.place
        for k in range(first, last):
            self.pairs[k].wait()
            for quarter in range(4):
                self.a[quarter, k] = (
                    self.g[here.core, k, quarter].astype(F32) + self.rc[k, quarter].astype(F32)
                ).astype(BF)
        span = pl.ds(first, last - first)
        for order in range(3):
            self.moves.append(
                self.copies.start(
                    self.a.at[here.members[order], span],
                    self.rx.at[order, span],
                    here.member(order),
                )
            )

    def along(self):
        here = self.place
        wait_all(self.moves)
        for k in range(here.zs):
            self.c[k] = (
                (self.a[here.gi, k].astype(F32) + self.rx[0, k].astype(F32))
                + (self.rx[1, k].astype(F32) + self.rx[2, k].astype(F32))
            ).astype(BF)
        self.moves = []
        for step in range(1, here.zs):
            there = lax.rem(here.z + step, here.zs)
            self.moves.append(
                self.copies.start(
                    self.c.at[there],
                    self.r3.at[step - 1],
                    {"group": here.gi, "patch": there * 2 + here.core},
                )
            )

    def share(self):
        here = self.place
        wait_all(self.moves)
        total = self.c[here.z].astype(F32)
        for step in range(1, here.zs):
            total += self.r3[step - 1].astype(F32)
        self.f[here.gi] = total.astype(BF)
        mine = self.f.at[here.gi]
        self.moves = [self.copies.start(mine, mine, here.member(order)) for order in range(3)]

    def finish(self, out):
        wait_all(self.moves)
        out[...] = self.f[...]


COUNT_SHARES = 7


def kernel(sizes, *refs):
    n_group, n_patch, padded, tile, tile_edges, fused, depths = sizes
    refs = list(refs)

    def take(count):
        got = refs[:count]
        del refs[:count]
        return got

    stored = take(14)
    edge_out, node_out = take(2)
    sums = take(3 if fused else 5)
    loaded = take(14)
    node, list_in, send_tiles, recv_tiles, edge, w_ei, w_eo, gain_e = loaded[:8]
    w_ni, w_no, gain_n, node_cot, edge_cot, count = loaded[8:]
    edge_grad, node_grad, load_sems, store_sems = take(4)
    send_col, send_row, recv_col, recv_row, list_col, list_row = take(6)
    outgoing, incoming, spread, returned = take(4)
    x_s, x_r, e_first, hidden, normed, inverse, message, joined = take(8)
    n_hidden, n_first, g_second, g_first, acc, gj, ge_second, ge_first, gs, gr, gains = take(11)
    send_sems, recv_sems = take(2)
    nodes, width = node.shape
    edges = edge.shape[0]
    halo = n_patch * padded
    place = Place(n_patch)
    gi, p = place.gi, place.p
    copies = Copies(send_sems, recv_sems)
    barrier = pltpu.get_barrier_semaphore()
    peers = [{"group": gi, "patch": lax.rem(p + d, n_patch)} for d in range(1, n_patch)]
    greeted = list(peers)
    if fused:
        greeted += [place.member(order) for order in range(3)]
    for peer in greeted:
        pl.semaphore_signal(barrier, inc=1, device_id=peer, device_id_type=MESH)
    loads = [
        pltpu.make_async_copy(source, target, load_sems.at[order])
        for order, (source, target) in enumerate(zip(stored, loaded))
    ]
    for load in loads:
        load.start()

    def column_of(line, column):
        for order in range(column.shape[0] // LANES):
            span = slice(order * LANES, (order + 1) * LANES)
            wide = jnp.broadcast_to(line[:, span].astype(F32), (8, LANES))
            column[span, :] = jnp.transpose(wide)[:, :1].astype(jnp.int32)

    loads[1].wait()
    list_row[...] = list_in[...]
    column_of(list_row, list_col)
    loads[0].wait()
    chosen = dot(hot(list_col[:halo, :], (halo, nodes), 1, 0), node[...]).astype(BF)
    outgoing[...] = chosen.reshape(n_patch, padded, width)
    pl.semaphore_wait(barrier, len(greeted))
    moving = [
        copies.start(outgoing.at[lax.rem(p + d, n_patch)], incoming.at[p], peers[d - 1])
        for d in range(1, n_patch)
    ]
    incoming[p] = outgoing[p]
    gains[...] = jnp.zeros_like(gains)

    loads[2].wait()
    loads[3].wait()
    for tiles, column, line in ((send_tiles, send_col, send_row), (recv_tiles, recv_col, recv_row)):
        turned = jnp.transpose(tiles[...].astype(F32)).astype(jnp.int32)
        for order in range(line.shape[1] // LANES):
            span = slice(order * LANES, (order + 1) * LANES)
            column[span, :] = turned[:, order : order + 1]
            line[:, span] = tiles[order : order + 1, :]

    loads[4].wait()
    loads[5].wait()

    def rows_of(k):
        return pl.ds(pl.multiple_of(k * tile, tile), tile)

    edge_tiles, node_tiles = edges // tile, nodes // tile

    @pl.loop(0, edge_tiles, unroll=fused)
    def _(k):
        rows = rows_of(k)
        latent = dot(hot(recv_col[rows, :], (tile, nodes), 1, 0), node[...]).astype(BF)
        x_r[rows, :] = latent
        e_first[rows, :] = dot(edge[rows, :], w_ei[:width, :]) + dot(latent, w_ei[2 * width :, :])


    @pl.loop(0, edge_tiles, unroll=fused)
    def _(k):
        rows = rows_of(k)
        x_s[rows, :] = dot(hot(send_col[rows, :], (tile, nodes), 1, 0), node[...]).astype(BF)

    loads[8].wait()

    @pl.loop(0, node_tiles, unroll=fused)
    def _(k):
        rows = rows_of(k)
        n_first[rows, :] = dot(node[rows, :], w_ni[:width, :])

    for load in loads[6:8] + loads[9:]:
        load.wait()
    wait_all(moving)

    def live_of(k):
        slot = lax.broadcasted_iota(jnp.int32, (tile, 1), 0) + k * tile
        return jnp.where(slot < count[0] * tile_edges, 1.0, 0.0)


    @pl.loop(0, edge_tiles, unroll=fused)
    def _(k):
        rows = rows_of(k)
        latent = dot(
            hot(send_col[rows, :], (tile, halo), 1, nodes), incoming[...].reshape(halo, width)
        )
        latent = x_s[rows, :] + latent.astype(BF)
        x_s[rows, :] = latent
        first = e_first[rows, :] + dot(latent, w_ei[width : 2 * width, :])
        active, slope = silu_pair(first)
        e_first[rows, :] = slope
        hid = active.astype(BF)
        hidden[rows, :] = hid
        norm, inv = normalize(dot(hid, w_eo[...]))
        normed[rows, :] = norm
        inverse[rows, :] = inv
        message[rows, :] = (live_of(k) * (gain_e[...] * norm)).astype(BF)


    @pl.loop(0, node_tiles, unroll=fused)
    def _(k):
        rows = rows_of(k)
        got = dot(hot(recv_row[...], (tile, edges), 0, k * tile), message[...]).astype(BF)
        joined[rows, :] = got
        first = n_first[rows, :] + dot(got, w_ni[width:, :])
        active, slope = silu_pair(first)
        hid = active.astype(BF)
        n_hidden[rows, :] = hid
        norm, inv = normalize(dot(hid, w_no[...]))
        up = node_cot[rows, :].astype(F32)
        gains[1:2, :] += jnp.sum(up * norm, axis=0, keepdims=True)
        second = normalize_back(up * gain_n[...], norm, inv).astype(BF)
        g_second[rows, :] = second
        grad = (dot_rt(second, w_no[...]) * slope).astype(BF)
        g_first[rows, :] = grad
        acc[rows, :] = up + dot_rt(grad, w_ni[:width, :])
        gj[rows, :] = dot_rt(grad, w_ni[width:, :]).astype(BF)

    def edge_back(k):
        rows = rows_of(k)
        taken = dot(hot(recv_col[rows, :], (tile, nodes), 1, 0), gj[...])
        live = live_of(k)
        norm = normed[rows, :]
        grad = live * (edge_cot[rows, :].astype(F32) + taken)
        gains[0:1, :] += jnp.sum(grad * norm, axis=0, keepdims=True)
        second = normalize_back(grad * gain_e[...], norm, inverse[rows, :]).astype(BF)
        ge_second[rows, :] = second
        ge_first[rows, :] = (dot_rt(second, w_eo[...]) * e_first[rows, :]).astype(BF)

    def rows_product(sources, start, stop, right):
        parts = []
        for order, source in enumerate(sources):
            low = max(start, order * width) - order * width
            high = min(stop, (order + 1) * width) - order * width
            if low < high:
                parts.append(dot_lt(source[:, low:high], right))
        return parts[0] if len(parts) == 1 else jnp.concatenate(parts, axis=0)

    if fused:
        zs = place.zs
        d_ei, d_eo, d_ni, d_no = depths
        red_n = Reduction(copies, take(COUNT_SHARES), place)
        red_e = Reduction(copies, take(COUNT_SHARES), place)
        red_o = Reduction(copies, take(COUNT_SHARES), place)
        for k in range(zs):
            start = 2 * k * d_ni
            red_n.put(
                k, 0, d_ni, rows_product((node, joined), start, start + 2 * d_ni, g_first[...])
            )
            red_n.put(
                k,
                d_ni,
                d_no,
                dot_lt(n_hidden[:, 2 * k * d_no : 2 * (k + 1) * d_no], g_second[...]),
            )
            red_n.pair(k)
            if k == zs - 2:
                red_n.spread(0, zs // 2)
        pl.loop(0, edge_tiles // 2, unroll=True)(edge_back)
        red_n.spread(zs // 2, zs)
        pl.loop(edge_tiles // 2, edge_tiles, unroll=True)(edge_back)
        for k in range(zs):
            start = 2 * k * d_ei
            red_e.put(
                k, 0, d_ei, rows_product((edge, x_s, x_r), start, start + 2 * d_ei, ge_first[...])
            )
            red_e.pair(k)
        red_e.spread(0, zs // 2)
    else:
        o_ei, o_eo, o_ni, o_no, o_gain = sums
        o_ni[:width, :] = dot_lt(node[...], g_first[...])
        o_ni[width:, :] = dot_lt(joined[...], g_first[...])
        o_no[...] = dot_lt(n_hidden[...], g_second[...])
        pl.loop(0, edge_tiles)(edge_back)
        o_ei[:width, :] = dot_lt(edge[...], ge_first[...])
        o_ei[width : 2 * width, :] = dot_lt(x_s[...], ge_first[...])
        o_ei[2 * width :, :] = dot_lt(x_r[...], ge_first[...])
        o_eo[...] = dot_lt(hidden[...], ge_second[...])
        o_gain[...] = gains[...]

    @pl.loop(0, edge_tiles, unroll=fused)
    def _(k):
        rows = rows_of(k)
        gs[rows, :] = dot_rt(ge_first[rows, :], w_ei[width : 2 * width, :]).astype(BF)

    back = dot(hot(send_row[...], (halo, edges), 0, nodes), gs[...]).astype(BF)
    spread[...] = back.reshape(n_patch, padded, width)
    moving = [
        copies.start(spread.at[lax.rem(p + d, n_patch)], returned.at[p], peers[d - 1])
        for d in range(1, n_patch)
    ]
    returned[p] = spread[p]
    if fused:
        red_e.spread(zs // 2, zs)
        for k in range(zs):
            red_o.put(
                k, 0, d_eo, dot_lt(hidden[:, 2 * k * d_eo : 2 * (k + 1) * d_eo], ge_second[...])
            )
            total = gains[...]
            red_o.put(k, d_eo, PACK, jnp.concatenate([total, total], axis=0))
            red_o.pair(k)

    @pl.loop(0, edge_tiles, unroll=fused)
    def _(k):
        rows = rows_of(k)
        gr[rows, :] = dot_rt(ge_first[rows, :], w_ei[2 * width :, :]).astype(BF)

    if fused:
        red_o.spread(0, zs)

    @pl.loop(0, edge_tiles, unroll=fused)
    def _(k):
        rows = rows_of(k)
        edge_grad[rows, :] = (
            live_of(k) * edge_cot[rows, :].astype(F32) + dot_rt(ge_first[rows, :], w_ei[:width, :])
        ).astype(BF)

    stores = [pltpu.make_async_copy(edge_grad, edge_out, store_sems.at[0])]
    stores[0].start()

    def gather_back(k):
        rows = rows_of(k)
        acc[rows, :] += dot(hot(send_row[...], (tile, edges), 0, k * tile), gs[...]) + dot(
            hot(recv_row[...], (tile, edges), 0, k * tile), gr[...]
        )

    if fused:
        red_n.along()
    pl.loop(0, node_tiles, unroll=fused)(gather_back)
    if fused:
        red_e.along()
        red_o.along()
    wait_all(moving)

    @pl.loop(0, node_tiles, unroll=fused)
    def _(k):
        rows = rows_of(k)
        node_grad[rows, :] = (
            acc[rows, :]
            + dot(
                hot(list_row[:, :halo], (tile, halo), 0, k * tile),
                returned[...].reshape(halo, width),
            )
        ).astype(BF)

    stores.append(pltpu.make_async_copy(node_grad, node_out, store_sems.at[1]))
    stores[1].start()
    if fused:
        red_n.share()
        red_e.share()
        red_o.share()
        red_n.finish(sums[0])
        red_e.finish(sums[1])
        red_o.finish(sums[2])
    for store in stores:
        store.wait()


def closing(factor, depths, *refs):
    edge_in, node_in, sum_n, sum_e, sum_o = refs[:5]
    edge_out, node_out, o_ei, o_eo, o_gain_e, o_ni, o_no, o_gain_n = refs[5:13]
    edge_hold, node_hold, load_sems, store_sems = refs[13:]
    d_ei, d_eo, d_ni, d_no = depths
    moves = [(edge_in, edge_hold, edge_out), (node_in, node_hold, node_out)]
    loads = [
        pltpu.make_async_copy(source, hold, load_sems.at[order])
        for order, (source, hold, _) in enumerate(moves)
    ]
    for load in loads:
        load.start()
    for quarter in range(4):
        span = slice(quarter * LANES, (quarter + 1) * LANES)
        o_ni[:, span] = sum_n[quarter, :d_ni].astype(F32) * factor
        o_no[:, span] = sum_n[quarter, d_ni:].astype(F32) * factor
        o_ei[:, span] = sum_e[quarter].astype(F32) * factor
        o_eo[:, span] = sum_o[quarter, :d_eo].astype(F32) * factor
    piece = o_gain_e.shape[1]
    p = lax.axis_index("patch")
    own = jnp.zeros((PACK, piece), F32)
    for quarter in range(4):
        lane = lax.broadcasted_iota(jnp.int32, (LANES, piece), 0) + quarter * LANES
        want = lax.broadcasted_iota(jnp.int32, (LANES, piece), 1) + p * piece
        pick = jnp.where(lane == want, 1.0, 0.0).astype(BF)
        own += dot(sum_o[quarter, d_eo:], pick)
    o_gain_e[...] = own[0:1] * factor
    o_gain_n[...] = own[1:2] * factor
    stores = []
    for order, (_, hold, out) in enumerate(moves):
        loads[order].wait()
        stores.append(pltpu.make_async_copy(hold, out, store_sems.at[order]))
        stores[order].start()
    for store in stores:
        store.wait()


def reduction_scratch(zs, depth):
    shapes = (
        (2, zs, 4, depth),
        (zs, 4, depth),
        (4, zs, depth),
        (3, zs, depth),
        (zs, depth),
        (zs - 1, depth),
        (4, depth),
    )
    return [pltpu.VMEM(shape + (LANES,), BF) for shape in shapes]


def local(
    n_group,
    n_patch,
    node_tape,
    edge_tape,
    node_cot,
    edge_cot,
    w_edge_in,
    w_edge_out,
    gain_edge,
    w_node_in,
    w_node_out,
    gain_node,
    senders,
    receivers,
    tile_count,
    send_rows,
):
    nodes, width = node_tape.shape[1:]
    edges = edge_tape.shape[1]
    listed = send_rows.shape[1]
    peer_rows = listed // n_patch
    padded = -(-peer_rows // PACK) * PACK
    halo = n_patch * padded
    tile = min(2 * LANES, nodes, edges)
    factor = float(n_group * n_patch * edges) ** (-0.5)

    if padded != peer_rows:
        beyond = senders - nodes
        beyond = beyond // peer_rows * padded + beyond % peer_rows
        senders = jnp.where(senders < nodes, senders, nodes + beyond)
        send_rows = jnp.pad(
            send_rows.reshape(n_patch, peer_rows),
            ((0, 0), (0, padded - peer_rows)),
            constant_values=-1,
        ).reshape(1, halo)
    slots = -(-halo // LANES) * LANES
    if slots != halo:
        send_rows = jnp.pad(send_rows, ((0, 0), (0, slots - halo)), constant_values=-1)

    def lane_rows(index):
        rows = -(-index.size // LANES)
        full = -(-rows // 8) * 8
        if index.shape == (full, LANES):
            return index
        return jnp.pad(index.reshape(-1), (0, full * LANES - index.size)).reshape(full, LANES)

    weights = (w_edge_in, w_edge_out, w_node_in, w_node_out)
    depths = [w.shape[0] // n_patch for w in weights]
    zs = n_patch // 2
    fused = (
        n_group == 4
        and n_patch % 4 == 0
        and width == 4 * LANES
        and all(d % PACK == 0 and 2 * d % LANES == 0 for d in depths)
    )
    operands = (
        node_tape[0],
        send_rows,
        lane_rows(senders),
        lane_rows(receivers),
        edge_tape[0],
        w_edge_in,
        w_edge_out,
        gain_edge[None],
        w_node_in,
        w_node_out,
        gain_node[None],
        node_cot[0],
        edge_cot[0],
        tile_count,
    )
    scratch = [pltpu.VMEM(operand.shape, operand.dtype) for operand in operands[:-1]]
    scratch += [pltpu.SMEM(tile_count.shape, tile_count.dtype)]
    scratch += [
        pltpu.VMEM((edges, width), BF),
        pltpu.VMEM((nodes, width), BF),
        pltpu.SemaphoreType.DMA((len(operands),)),
        pltpu.SemaphoreType.DMA((2,)),
    ]
    for length in (edges, edges, slots):
        scratch += [pltpu.VMEM((length, 1), jnp.int32), pltpu.VMEM((1, length), jnp.int32)]
    scratch += [pltpu.VMEM((n_patch, padded, width), BF)] * 4
    by_edge, by_node = pltpu.VMEM((edges, width), BF), pltpu.VMEM((nodes, width), BF)
    wide_edge, wide_node = pltpu.VMEM((edges, width), F32), pltpu.VMEM((nodes, width), F32)
    scratch += [by_edge, by_edge, wide_edge, by_edge, wide_edge, pltpu.VMEM((edges, 1), F32)]
    scratch += [by_edge, by_node]
    scratch += [by_node, wide_node, by_node, by_node, wide_node, by_node]
    scratch += [by_edge, by_edge, by_edge, by_edge, pltpu.VMEM((PACK, width), F32)]
    n_copies = 2 * (n_patch - 1)
    d_ei, d_eo, d_ni, d_no = depths
    reductions = []
    if fused:
        for depth, halves in ((d_ni + d_no, 2), (d_ei, 2), (d_eo + PACK, 1)):
            reductions += reduction_scratch(zs, depth)
            n_copies += zs + 3 * halves + zs - 1 + 3
        summed_shapes = [
            jax.ShapeDtypeStruct((4, depth, LANES), BF)
            for depth in (d_ni + d_no, d_ei, d_eo + PACK)
        ]
    else:
        summed_shapes = [jax.ShapeDtypeStruct((w.shape[0], width), F32) for w in weights]
        summed_shapes += [jax.ShapeDtypeStruct((PACK, width), F32)]
    scratch += [pltpu.SemaphoreType.DMA((n_copies,)), pltpu.SemaphoreType.DMA((n_copies,))]
    scratch += reductions

    vmem = pl.BlockSpec(memory_space=pltpu.VMEM)
    anywhere = pl.BlockSpec(memory_space=pl.ANY)
    sizes = (n_group, n_patch, padded, tile, senders.shape[1], fused, depths)
    edge_grad, node_grad, *sums = pl.pallas_call(
        functools.partial(kernel, sizes),
        out_shape=[
            jax.ShapeDtypeStruct((edges, width), BF),
            jax.ShapeDtypeStruct((nodes, width), BF),
        ]
        + summed_shapes,
        in_specs=[anywhere] * len(operands),
        out_specs=[anywhere] * 2 + [vmem] * len(summed_shapes),
        scratch_shapes=scratch,
        compiler_params=pltpu.CompilerParams(
            collective_id=0, has_side_effects=True, vmem_limit_bytes=63 * 1024 * 1024
        ),
    )(*operands)
    if fused:
        piece = width // n_patch
        rows_out = [jax.ShapeDtypeStruct((depth, width), F32) for depth in depths]
        gain_out = jax.ShapeDtypeStruct((1, piece), F32)
        o_ei, o_eo, o_ni, o_no = rows_out
        edge_grad, node_grad, o_ei, o_eo, gain_e, o_ni, o_no, gain_n = pl.pallas_call(
            functools.partial(closing, factor, depths),
            out_shape=[
                jax.ShapeDtypeStruct((edges, width), BF),
                jax.ShapeDtypeStruct((nodes, width), BF),
                o_ei,
                o_eo,
                gain_out,
                o_ni,
                o_no,
                gain_out,
            ],
            in_specs=[anywhere] * 2 + [vmem] * 3,
            out_specs=[anywhere] * 2 + [vmem] * 6,
            scratch_shapes=[
                pltpu.VMEM((edges, width), BF),
                pltpu.VMEM((nodes, width), BF),
                pltpu.SemaphoreType.DMA((2,)),
                pltpu.SemaphoreType.DMA((2,)),
            ],
            compiler_params=pltpu.CompilerParams(vmem_limit_bytes=16 * 1024 * 1024),
        )(edge_grad, node_grad, *sums)
        return (
            edge_grad[None],
            node_grad[None],
            o_ei,
            o_eo,
            gain_e.reshape(piece),
            o_ni,
            o_no,
            gain_n.reshape(piece),
        )
    p_ei, p_eo, p_ni, p_no, p_gain = sums

    def summed(value):
        part = lax.psum_scatter(value, "patch", scatter_dimension=0, tiled=True)
        return lax.psum(part.astype(BF), "group").astype(F32) * factor

    return (
        edge_grad[None],
        node_grad[None],
        summed(p_ei),
        summed(p_eo),
        summed(p_gain[0]),
        summed(p_ni),
        summed(p_no),
        summed(p_gain[1]),
    )


def solution(mesh):
    member = P("group", "patch", None)
    placed = (member,) * 4 + (P(),) * 6
    placed += (P("patch", None), P("patch", None), P("patch"), P("patch", None))
    rows = P("patch", None)
    return jax.shard_map(
        functools.partial(local, mesh.shape["group"], mesh.shape["patch"]),
        mesh=mesh,
        in_specs=placed,
        out_specs=(member, member, rows, rows, P("patch"), rows, rows, P("patch")),
        check_vma=False,
    )
```

time: 83.9 us -> 66.6 us (0.79)
  Pallas kernels: 73.7 us -> 59.7 us
  local copies, waits for them, and re-layouts: 8.62 us -> 5.18 us
    pallas_call x1, Pallas kernels: 73.7 us -> 57 us  [local(): pl.pallas_call(functools.partial(kernel, sizes), out_shape=[jax.ShapeDtyp...]
    pallas_call x0 -> x1, Pallas kernels: none -> 2.68 us  [local(): pl.pallas_call(functools.partial(closing, factor, depths), out_shape=[jax...]
    squeeze x1 -> x0, local copies, waits for them, and re-layouts: 1.28 us -> none  [local(): p_gain[1]]
    reshape x1 -> x0, local copies, waits for them, and re-layouts: 1.27 us -> none  [tiles_of(): jnp.pad(index, (0, full * LANES - index.shape[0])).reshape(full, LANES)]
    unnamed x16 -> x10, local copies, waits for them, and re-layouts: 6.06 us -> 5.18 us
where the time goes in v1:
time: 66.6 us; the launch traced here: 66.3 us
  Pallas kernels  59.7 us (90%)
  local copies, waits for them, and re-layouts  5.18 us (8%)
  between operations  1.47 us (2%)
    pallas_call x1, Pallas kernels, local(): pl.pallas_call(functools.partial(kernel, sizes), out_shape=[jax.ShapeDtyp...  57 us
    unnamed x10, local copies, waits for them, and re-layouts  5.18 us
    pallas_call x1, Pallas kernels, local(): pl.pallas_call(functools.partial(closing, factor, depths), out_shape=[jax...  2.68 us

profile of v1, /device:TPU:0, one launch (start us, length us, event | category | flops | bytes accessed | tf_op | source)
XLA Modules:
  0.0 66.3 jit_solution(15662406000428918427)
XLA Ops:
  1.3 57.0 %shard_map.197 = (bf16[1024,512]{1,0:T(8,128)(2,1)}, bf16[1024,512]{1,0:T(8,128)(2,1)}, bf16[4,192,128]{2,1,0:T(8,128)(2,1)}, bf16[4,192,128]{2,1,0:T(8,128)(2,1)}, bf16[4,80,128]{2,1,0:T(8,128)(2,1)}) custom-call(bf16[1024,512]{1,0:T(8,128)(2,1)} %bitcast.10, s32[1,256]{1,0:T(1,128)} %refs_1_.1, s32[8,128]{1,0:T(8,128)} %refs_2_.1, s32[8,128]{1,0:T(8,128)} %refs_3_.1, ...), custom_call_target="tpu_custom_call" | custom-call | tf_op jit(solution)/shard_map/pallas_call | solution.py:614
  58.3 0.0 copy-start
  58.3 1.2 %copy-done = bf16[1024,512]{1,0:T(8,128)(2,1)S(1)} copy-done((bf16[1024,512]{1,0:T(8,128)(2,1)S(1)}, bf16[1024,512]{1,0:T(8,128)(2,1)}, u32[]{:S(2)}) %copy-start) | copy-done | bytes 1048600
  59.5 0.0 copy-start.1
  59.5 1.2 %copy-done.1 = bf16[1024,512]{1,0:T(8,128)(2,1)S(1)} copy-done((bf16[1024,512]{1,0:T(8,128)(2,1)S(1)}, bf16[1024,512]{1,0:T(8,128)(2,1)}, u32[]{:S(2)}) %copy-start.1) | copy-done | bytes 1048600
  60.7 0.0 copy-start.2
  60.7 0.9 %copy-done.2 = bf16[4,192,128]{2,1,0:T(8,128)(2,1)S(1)} copy-done((bf16[4,192,128]{2,1,0:T(8,128)(2,1)S(1)}, bf16[4,192,128]{2,1,0:T(8,128)(2,1)}, u32[]{:S(2)}) %copy-start.2) | copy-done | bytes 196632
  61.7 0.0 copy-start.3
  61.7 0.9 %copy-done.3 = bf16[4,192,128]{2,1,0:T(8,128)(2,1)S(1)} copy-done((bf16[4,192,128]{2,1,0:T(8,128)(2,1)S(1)}, bf16[4,192,128]{2,1,0:T(8,128)(2,1)}, u32[]{:S(2)}) %copy-start.3) | copy-done | bytes 196632
  62.6 0.0 copy-start.4
  62.6 0.9 %copy-done.4 = bf16[4,80,128]{2,1,0:T(8,128)(2,1)S(1)} copy-done((bf16[4,80,128]{2,1,0:T(8,128)(2,1)S(1)}, bf16[4,80,128]{2,1,0:T(8,128)(2,1)}, u32[]{:S(2)}) %copy-start.4) | copy-done | bytes 81944
  63.5 2.7 %shard_map.198 = (bf16[1024,512]{1,0:T(8,128)(2,1)}, bf16[1024,512]{1,0:T(8,128)(2,1)}, f32[192,512]{1,0:T(8,128)}, f32[64,512]{1,0:T(8,128)}, f32[1,64]{1,0:T(1...) custom-call(bf16[1024,512]{1,0:T(8,128)(2,1)S(1)} %copy-done, bf16[1024,512]{1,0:T(8,128)(2,1)S(1)} %copy-done.1, ...), custom_call_target="tpu_custom_call" | custom-call | tf_op jit(solution)/shard_map/pallas_call | solution.py:633
Async XLA Ops:
  58.3 1.2 %copy-start = (bf16[1024,512]{1,0:T(8,128)(2,1)S(1)}, bf16[1024,512]{1,0:T(8,128)(2,1)}, u32[]{:S(2)}) copy-start(bf16[1024,512]{1,0:T(8,128)(2,1)} %get-tuple-element.21.refs_0_) | copy-start | bytes 3145732
  59.5 1.2 %copy-start.1 = (bf16[1024,512]{1,0:T(8,128)(2,1)S(1)}, bf16[1024,512]{1,0:T(8,128)(2,1)}, u32[]{:S(2)}) copy-start(bf16[1024,512]{1,0:T(8,128)(2,1)} %get-tuple-element.22.refs_1_) | copy-start | bytes 3145732
  60.7 0.9 %copy-start.2 = (bf16[4,192,128]{2,1,0:T(8,128)(2,1)S(1)}, bf16[4,192,128]{2,1,0:T(8,128)(2,1)}, u32[]{:S(2)}) copy-start(bf16[4,192,128]{2,1,0:T(8,128)(2,1)} %get-tuple-element.23.refs_2_) | copy-start | bytes 589828
  61.7 0.9 %copy-start.3 = (bf16[4,192,128]{2,1,0:T(8,128)(2,1)S(1)}, bf16[4,192,128]{2,1,0:T(8,128)(2,1)}, u32[]{:S(2)}) copy-start(bf16[4,192,128]{2,1,0:T(8,128)(2,1)} %get-tuple-element.24.refs_3_) | copy-start | bytes 589828
  62.6 0.9 %copy-start.4 = (bf16[4,80,128]{2,1,0:T(8,128)(2,1)S(1)}, bf16[4,80,128]{2,1,0:T(8,128)(2,1)}, u32[]{:S(2)}) copy-start(bf16[4,80,128]{2,1,0:T(8,128)(2,1)} %get-tuple-element.25.refs_4_) | copy-start | bytes 245764

commit v2 on v1

--- a/solution.py
+++ b/solution.py
@@ -76,6 +76,33 @@
         copy.wait()
 
 
+def staggered(count, stages, hooks=None, unrolled=True):
+    if not unrolled:
+
+        @pl.loop(0, count)
+        def _(k):
+            held = None
+            for stage in stages:
+                held = stage(k, held)
+
+        return
+    held = {}
+    for step in range(count + len(stages) - 1):
+        for order in range(len(stages)):
+            k = step - order
+            if 0 <= k < count:
+                held[k] = stages[order](k, held.get(k))
+        if hooks and step in hooks:
+            hooks[step]()
+
+
+def flipped(index, bits):
+    for place in range(bits.bit_length()):
+        if bits >> place & 1:
+            index = index + (1 - 2 * lax.rem(lax.div(index, 1 << place), 2)) * (1 << place)
+    return index
+
+
 class Place:
     def __init__(self, n_patch):
         self.gi = lax.axis_index("group")
@@ -84,25 +111,28 @@
         self.z = lax.div(self.p, 2)
         self.zs = n_patch // 2
         self.partner = {"group": self.gi, "patch": self.p + 1 - 2 * self.core}
-        gx, gy = lax.rem(self.gi, 2), lax.div(self.gi, 2)
-        flip_x, flip_y = 1 - 2 * gx, 2 - 4 * gy
-        self.members = [self.gi + flip_x, self.gi + flip_y, self.gi + flip_x + flip_y]
-
-    def member(self, order):
-        return {"group": self.members[order], "patch": self.p}
+        self.gx, self.gy = lax.rem(self.gi, 2), lax.div(self.gi, 2)
+        flip_x, flip_y = 1 - 2 * self.gx, 2 - 4 * self.gy
+        self.members = [
+            {"group": self.gi + flip, "patch": self.p} for flip in (flip_x, flip_y, flip_x + flip_y)
+        ]
+        self.x_peer, self.y_peer = self.members[:2]
 
 
 class Reduction:
     def __init__(self, copies, refs, place):
         self.copies, self.place = copies, place
-        self.g, self.rc, self.a, self.rx, self.c, self.r3, self.f = refs
-        self.pairs, self.moves = [], []
+        self.g, self.rc, self.a, self.r1x, self.r1y, self.b0, self.b1 = refs[:7]
+        self.r2x, self.r2y, self.c, self.r3, self.f = refs[7:]
+        depth, middle = self.c.shape[1], self.r1x.shape[2]
+        self.low, self.high = pl.ds(0, middle), pl.ds(middle, depth - middle)
+        self.pairs, self.first, self.second = [], {}, []
 
     def put(self, k, row, size, value):
         value = value.astype(BF)
         for c in range(2):
             for quarter in range(4):
-                self.g[c, k, quarter, row : row + size, :] = value[
+                self.g[c, k, quarter // 2, quarter % 2, row : row + size, :] = value[
                     c * size : (c + 1) * size, quarter * LANES : (quarter + 1) * LANES
                 ]
 
@@ -112,31 +142,56 @@
             self.copies.start(self.g.at[1 - here.core, k], self.rc.at[k], here.partner)
         )
 
-    def spread(self, first, last):
+    def step1(self, first, last):
         here = self.place
         for k in range(first, last):
             self.pairs[k].wait()
-            for quarter in range(4):
-                self.a[quarter, k] = (
-                    self.g[here.core, k, quarter].astype(F32) + self.rc[k, quarter].astype(F32)
-                ).astype(BF)
+            for gy in range(2):
+                for gx in range(2):
+                    self.a[gy, gx, k] = (
+                        self.g[here.core, k, gy, gx].astype(F32) + self.rc[k, gy, gx].astype(F32)
+                    ).astype(BF)
         span = pl.ds(first, last - first)
-        for order in range(3):
-            self.moves.append(
-                self.copies.start(
-                    self.a.at[here.members[order], span],
-                    self.rx.at[order, span],
-                    here.member(order),
-                )
-            )
+        self.first[first] = [
+            self.copies.start(
+                self.a.at[:, 1 - here.gx, span, self.low], self.r1x.at[:, span], here.x_peer
+            ),
+            self.copies.start(
+                self.a.at[1 - here.gy, :, span, self.high], self.r1y.at[:, span], here.y_peer
+            ),
+        ]
+
+    def step2(self, first, last):
+        here = self.place
+        wait_all(self.first[first])
+        for k in range(first, last):
+            self.b0[k] = (
+                self.a[1 - here.gy, here.gx, k, self.low].astype(F32)
+                + self.r1x[1 - here.gy, k].astype(F32)
+            ).astype(BF)
+            self.b1[k] = (
+                self.a[here.gy, 1 - here.gx, k, self.high].astype(F32)
+                + self.r1y[1 - here.gx, k].astype(F32)
+            ).astype(BF)
+        span = pl.ds(first, last - first)
+        self.second += [
+            self.copies.start(self.b0.at[span], self.r2y.at[span], here.y_peer),
+            self.copies.start(self.b1.at[span], self.r2x.at[span], here.x_peer),
+        ]
 
     def along(self):
         here = self.place
-        wait_all(self.moves)
+        wait_all(self.second)
         for k in range(here.zs):
-            self.c[k] = (
-                (self.a[here.gi, k].astype(F32) + self.rx[0, k].astype(F32))
-                + (self.rx[1, k].astype(F32) + self.rx[2, k].astype(F32))
+            self.c[k, self.low] = (
+                self.a[here.gy, here.gx, k, self.low].astype(F32)
+                + self.r1x[here.gy, k].astype(F32)
+                + self.r2y[k].astype(F32)
+            ).astype(BF)
+            self.c[k, self.high] = (
+                self.a[here.gy, here.gx, k, self.high].astype(F32)
+                + self.r1y[here.gx, k].astype(F32)
+                + self.r2x[k].astype(F32)
             ).astype(BF)
         self.moves = []
         for step in range(1, here.zs):
@@ -157,14 +212,14 @@
             total += self.r3[step - 1].astype(F32)
         self.f[here.gi] = total.astype(BF)
         mine = self.f.at[here.gi]
-        self.moves = [self.copies.start(mine, mine, here.member(order)) for order in range(3)]
+        self.moves = [self.copies.start(mine, mine, member) for member in here.members]
 
     def finish(self, out):
         wait_all(self.moves)
         out[...] = self.f[...]
 
 
-COUNT_SHARES = 7
+COUNT_SHARES = 12
 
 
 def kernel(sizes, *refs):
@@ -182,7 +237,8 @@
     loaded = take(14)
     node, list_in, send_tiles, recv_tiles, edge, w_ei, w_eo, gain_e = loaded[:8]
     w_ni, w_no, gain_n, node_cot, edge_cot, count = loaded[8:]
-    edge_grad, node_grad, load_sems, store_sems = take(4)
+    edge_grad, node_grad = (edge_out, node_out) if fused else take(2)
+    load_sems, store_sems = take(2)
     send_col, send_row, recv_col, recv_row, list_col, list_row = take(6)
     outgoing, incoming, spread, returned = take(4)
     x_s, x_r, e_first, hidden, normed, inverse, message, joined = take(8)
@@ -195,10 +251,14 @@
     gi, p = place.gi, place.p
     copies = Copies(send_sems, recv_sems)
     barrier = pltpu.get_barrier_semaphore()
-    peers = [{"group": gi, "patch": lax.rem(p + d, n_patch)} for d in range(1, n_patch)]
+    if fused and n_patch & (n_patch - 1) == 0:
+        others = [flipped(p, d) for d in range(n_patch - 1, 0, -1)]
+    else:
+        others = [lax.rem(p + d, n_patch) for d in range(1, n_patch)]
+    peers = [{"group": gi, "patch": other} for other in others]
     greeted = list(peers)
     if fused:
-        greeted += [place.member(order) for order in range(3)]
+        greeted += place.members
     for peer in greeted:
         pl.semaphore_signal(barrier, inc=1, device_id=peer, device_id_type=MESH)
     loads = [
@@ -222,8 +282,8 @@
     outgoing[...] = chosen.reshape(n_patch, padded, width)
     pl.semaphore_wait(barrier, len(greeted))
     moving = [
-        copies.start(outgoing.at[lax.rem(p + d, n_patch)], incoming.at[p], peers[d - 1])
-        for d in range(1, n_patch)
+        copies.start(outgoing.at[other], incoming.at[p], peer)
+        for other, peer in zip(others, peers)
     ]
     incoming[p] = outgoing[p]
     gains[...] = jnp.zeros_like(gains)
@@ -240,88 +300,118 @@
     loads[4].wait()
     loads[5].wait()
 
-    def rows_of(k):
-        return pl.ds(pl.multiple_of(k * tile, tile), tile)
+    def rows_of(k, size=tile):
+        return pl.ds(k * size if isinstance(k, int) else pl.multiple_of(k * size, size), size)
+
+    long = 2 * tile if fused and edges % (2 * tile) == 0 and nodes % (2 * tile) == 0 else tile
 
     edge_tiles, node_tiles = edges // tile, nodes // tile
 
-    @pl.loop(0, edge_tiles, unroll=fused)
+    @pl.loop(0, edges // long, unroll=fused)
     def _(k):
-        rows = rows_of(k)
-        latent = dot(hot(recv_col[rows, :], (tile, nodes), 1, 0), node[...]).astype(BF)
+        rows = rows_of(k, long)
+        latent = dot(hot(recv_col[rows, :], (long, nodes), 1, 0), node[...]).astype(BF)
         x_r[rows, :] = latent
         e_first[rows, :] = dot(edge[rows, :], w_ei[:width, :]) + dot(latent, w_ei[2 * width :, :])
 
 
-    @pl.loop(0, edge_tiles, unroll=fused)
+    @pl.loop(0, edges // long, unroll=fused)
     def _(k):
-        rows = rows_of(k)
-        x_s[rows, :] = dot(hot(send_col[rows, :], (tile, nodes), 1, 0), node[...]).astype(BF)
+        rows = rows_of(k, long)
+        x_s[rows, :] = dot(hot(send_col[rows, :], (long, nodes), 1, 0), node[...]).astype(BF)
 
     loads[8].wait()
 
-    @pl.loop(0, node_tiles, unroll=fused)
+    @pl.loop(0, nodes // long, unroll=fused)
     def _(k):
-        rows = rows_of(k)
+        rows = rows_of(k, long)
         n_first[rows, :] = dot(node[rows, :], w_ni[:width, :])
 
     for load in loads[6:8] + loads[9:]:
         load.wait()
     wait_all(moving)
 
-    def live_of(k):
-        slot = lax.broadcasted_iota(jnp.int32, (tile, 1), 0) + k * tile
-        return jnp.where(slot < count[0] * tile_edges, 1.0, 0.0)
-
-
-    @pl.loop(0, edge_tiles, unroll=fused)
-    def _(k):
+    def live_of(k, size=tile):
+        slot = lax.broadcasted_iota(jnp.int32, (size, 1), 0) + k * size
+        return jnp.where(slot < count[...] * tile_edges, 1.0, 0.0)
+
+
+    def edge_first(k, _):
         rows = rows_of(k)
         latent = dot(
             hot(send_col[rows, :], (tile, halo), 1, nodes), incoming[...].reshape(halo, width)
         )
         latent = x_s[rows, :] + latent.astype(BF)
         x_s[rows, :] = latent
-        first = e_first[rows, :] + dot(latent, w_ei[width : 2 * width, :])
+        return e_first[rows, :] + dot(latent, w_ei[width : 2 * width, :])
+
+    def edge_hidden(k, first):
+        rows = rows_of(k)
         active, slope = silu_pair(first)
         e_first[rows, :] = slope
         hid = active.astype(BF)
         hidden[rows, :] = hid
-        norm, inv = normalize(dot(hid, w_eo[...]))
+        return dot(hid, w_eo[...])
+
+    def edge_message(k, second):
+        rows = rows_of(k)
+        norm, inv = normalize(second)
         normed[rows, :] = norm
         inverse[rows, :] = inv
         message[rows, :] = (live_of(k) * (gain_e[...] * norm)).astype(BF)
 
-
-    @pl.loop(0, node_tiles, unroll=fused)
-    def _(k):
+    staggered(edge_tiles, (edge_first, edge_hidden, edge_message), unrolled=fused)
+
+    def node_first(k, _):
         rows = rows_of(k)
         got = dot(hot(recv_row[...], (tile, edges), 0, k * tile), message[...]).astype(BF)
         joined[rows, :] = got
-        first = n_first[rows, :] + dot(got, w_ni[width:, :])
+        return n_first[rows, :] + dot(got, w_ni[width:, :])
+
+    def node_hidden(k, first):
+        rows = rows_of(k)
         active, slope = silu_pair(first)
         hid = active.astype(BF)
         n_hidden[rows, :] = hid
-        norm, inv = normalize(dot(hid, w_no[...]))
+        return (slope, dot(hid, w_no[...]))
+
+    def node_second(k, held):
+        slope, second = held
+        rows = rows_of(k)
+        norm, inv = normalize(second)
         up = node_cot[rows, :].astype(F32)
         gains[1:2, :] += jnp.sum(up * norm, axis=0, keepdims=True)
         second = normalize_back(up * gain_n[...], norm, inv).astype(BF)
         g_second[rows, :] = second
-        grad = (dot_rt(second, w_no[...]) * slope).astype(BF)
+        return (slope, dot_rt(second, w_no[...]))
+
+    def node_back(k, held):
+        slope, grad = held
+        rows = rows_of(k)
+        grad = (grad * slope).astype(BF)
         g_first[rows, :] = grad
-        acc[rows, :] = up + dot_rt(grad, w_ni[:width, :])
+        acc[rows, :] = node_cot[rows, :].astype(F32) + dot_rt(grad, w_ni[:width, :])
         gj[rows, :] = dot_rt(grad, w_ni[width:, :]).astype(BF)
 
-    def edge_back(k):
-        rows = rows_of(k)
-        taken = dot(hot(recv_col[rows, :], (tile, nodes), 1, 0), gj[...])
-        live = live_of(k)
+    staggered(node_tiles, (node_first, node_hidden, node_second, node_back), unrolled=fused)
+
+    def edge_taken(k, _):
+        return dot(hot(recv_col[rows_of(k), :], (tile, nodes), 1, 0), gj[...])
+
+    def edge_second(k, taken):
+        rows = rows_of(k)
         norm = normed[rows, :]
-        grad = live * (edge_cot[rows, :].astype(F32) + taken)
+        grad = live_of(k) * (edge_cot[rows, :].astype(F32) + taken)
         gains[0:1, :] += jnp.sum(grad * norm, axis=0, keepdims=True)
         second = normalize_back(grad * gain_e[...], norm, inverse[rows, :]).astype(BF)
         ge_second[rows, :] = second
-        ge_first[rows, :] = (dot_rt(second, w_eo[...]) * e_first[rows, :]).astype(BF)
+        return dot_rt(second, w_eo[...])
+
+    def edge_back(k, grad):
+        rows = rows_of(k)
+        ge_first[rows, :] = (grad * e_first[rows, :]).astype(BF)
+
+    edge_stages = (edge_taken, edge_second, edge_back)
 
     def rows_product(sources, start, stop, right):
         parts = []
@@ -334,98 +424,109 @@
 
     if fused:
         zs = place.zs
+        half = zs // 2
         d_ei, d_eo, d_ni, d_no = depths
         red_n = Reduction(copies, take(COUNT_SHARES), place)
         red_e = Reduction(copies, take(COUNT_SHARES), place)
         red_o = Reduction(copies, take(COUNT_SHARES), place)
+        for first in (0, half):
+            for k in range(first, first + half):
+                start = 2 * k * d_ni
+                value = rows_product((node, joined), start, start + 2 * d_ni, g_first[...])
+                red_n.put(k, 0, d_ni, value)
+                value = dot_lt(n_hidden[:, 2 * k * d_no : 2 * (k + 1) * d_no], g_second[...])
+                red_n.put(k, d_ni, d_no, value)
+            for k in range(first, first + half):
+                red_n.pair(k)
+        red_n.step1(0, half)
+        staggered(edge_tiles, edge_stages, hooks={2: lambda: red_n.step1(half, zs)})
+        for first in (0, half):
+            for k in range(first, first + half):
+                start = 2 * k * d_ei
+                value = rows_product((edge, x_s, x_r), start, start + 2 * d_ei, ge_first[...])
+                red_e.put(k, 0, d_ei, value)
+            for k in range(first, first + half):
+                red_e.pair(k)
+            if first == 0:
+                red_n.step2(0, half)
+        red_e.step1(0, half)
+        red_n.step2(half, zs)
+        total = gains[...].astype(BF)
+        total = jnp.concatenate([total, total], axis=0)
         for k in range(zs):
-            start = 2 * k * d_ni
-            red_n.put(
-                k, 0, d_ni, rows_product((node, joined), start, start + 2 * d_ni, g_first[...])
+            red_o.put(
+                k, 0, d_eo, dot_lt(hidden[:, 2 * k * d_eo : 2 * (k + 1) * d_eo], ge_second[...])
             )
-            red_n.put(
-                k,
-                d_ni,
-                d_no,
-                dot_lt(n_hidden[:, 2 * k * d_no : 2 * (k + 1) * d_no], g_second[...]),
-            )
-            red_n.pair(k)
-            if k == zs - 2:
-                red_n.spread(0, zs // 2)
-        pl.loop(0, edge_tiles // 2, unroll=True)(edge_back)
-        red_n.spread(zs // 2, zs)
-        pl.loop(edge_tiles // 2, edge_tiles, unroll=True)(edge_back)
+            red_o.put(k, d_eo, PACK, total)
         for k in range(zs):
-            start = 2 * k * d_ei
-            red_e.put(
-                k, 0, d_ei, rows_product((edge, x_s, x_r), start, start + 2 * d_ei, ge_first[...])
-            )
-            red_e.pair(k)
-        red_e.spread(0, zs // 2)
+            red_o.pair(k)
+        red_e.step1(half, zs)
     else:
         o_ei, o_eo, o_ni, o_no, o_gain = sums
         o_ni[:width, :] = dot_lt(node[...], g_first[...])
         o_ni[width:, :] = dot_lt(joined[...], g_first[...])
         o_no[...] = dot_lt(n_hidden[...], g_second[...])
-        pl.loop(0, edge_tiles)(edge_back)
+        staggered(edge_tiles, edge_stages, unrolled=False)
         o_ei[:width, :] = dot_lt(edge[...], ge_first[...])
         o_ei[width : 2 * width, :] = dot_lt(x_s[...], ge_first[...])
         o_ei[2 * width :, :] = dot_lt(x_r[...], ge_first[...])
         o_eo[...] = dot_lt(hidden[...], ge_second[...])
         o_gain[...] = gains[...]
 
-    @pl.loop(0, edge_tiles, unroll=fused)
+    @pl.loop(0, edges // long, unroll=fused)
     def _(k):
-        rows = rows_of(k)
+        rows = rows_of(k, long)
         gs[rows, :] = dot_rt(ge_first[rows, :], w_ei[width : 2 * width, :]).astype(BF)
 
     back = dot(hot(send_row[...], (halo, edges), 0, nodes), gs[...]).astype(BF)
     spread[...] = back.reshape(n_patch, padded, width)
     moving = [
-        copies.start(spread.at[lax.rem(p + d, n_patch)], returned.at[p], peers[d - 1])
-        for d in range(1, n_patch)
+        copies.start(spread.at[other], returned.at[p], peer)
+        for other, peer in zip(others, peers)
     ]
     returned[p] = spread[p]
     if fused:
-        red_e.spread(zs // 2, zs)
-        for k in range(zs):
-            red_o.put(
-                k, 0, d_eo, dot_lt(hidden[:, 2 * k * d_eo : 2 * (k + 1) * d_eo], ge_second[...])
-            )
-            total = gains[...]
-            red_o.put(k, d_eo, PACK, jnp.concatenate([total, total], axis=0))
-            red_o.pair(k)
-
-    @pl.loop(0, edge_tiles, unroll=fused)
+        red_o.step1(0, zs)
+
+    @pl.loop(0, edges // long, unroll=fused)
     def _(k):
-        rows = rows_of(k)
+        rows = rows_of(k, long)
         gr[rows, :] = dot_rt(ge_first[rows, :], w_ei[2 * width :, :]).astype(BF)
 
     if fused:
-        red_o.spread(0, zs)
-
-    @pl.loop(0, edge_tiles, unroll=fused)
+        red_n.along()
+
+    @pl.loop(0, edges // long, unroll=fused)
     def _(k):
-        rows = rows_of(k)
+        rows = rows_of(k, long)
         edge_grad[rows, :] = (
-            live_of(k) * edge_cot[rows, :].astype(F32) + dot_rt(ge_first[rows, :], w_ei[:width, :])
+            live_of(k, long) * edge_cot[rows, :].astype(F32)
+            + dot_rt(ge_first[rows, :], w_ei[:width, :])
         ).astype(BF)
 
-    stores = [pltpu.make_async_copy(edge_grad, edge_out, store_sems.at[0])]
-    stores[0].start()
+    stores = []
+    if not fused:
+        stores.append(pltpu.make_async_copy(edge_grad, edge_out, store_sems.at[0]))
+        stores[0].start()
 
     def gather_back(k):
-        rows = rows_of(k)
-        acc[rows, :] += dot(hot(send_row[...], (tile, edges), 0, k * tile), gs[...]) + dot(
-            hot(recv_row[...], (tile, edges), 0, k * tile), gr[...]
+        rows = rows_of(k, long)
+        acc[rows, :] += dot(hot(send_row[...], (long, edges), 0, k * long), gs[...]) + dot(
+            hot(recv_row[...], (long, edges), 0, k * long), gr[...]
         )
 
     if fused:
-        red_n.along()
-    pl.loop(0, node_tiles, unroll=fused)(gather_back)
+        red_e.step2(0, half)
+    gathers = nodes // long
+    pl.loop(0, gathers // 2, unroll=fused)(gather_back)
+    if fused:
+        red_e.step2(half, zs)
+        red_o.step2(0, zs)
+    pl.loop(gathers // 2, gathers, unroll=fused)(gather_back)
     if fused:
         red_e.along()
         red_o.along()
+        red_n.share()
     wait_all(moving)
 
     @pl.loop(0, node_tiles, unroll=fused)
@@ -439,10 +540,10 @@
             )
         ).astype(BF)
 
-    stores.append(pltpu.make_async_copy(node_grad, node_out, store_sems.at[1]))
-    stores[1].start()
-    if fused:
-        red_n.share()
+    if not fused:
+        stores.append(pltpu.make_async_copy(node_grad, node_out, store_sems.at[1]))
+        stores[1].start()
+    if fused:
         red_e.share()
         red_o.share()
         red_n.finish(sums[0])
@@ -454,22 +555,27 @@
 
 def closing(factor, depths, *refs):
     edge_in, node_in, sum_n, sum_e, sum_o = refs[:5]
-    edge_out, node_out, o_ei, o_eo, o_gain_e, o_ni, o_no, o_gain_n = refs[5:13]
-    edge_hold, node_hold, load_sems, store_sems = refs[13:]
+    outs = refs[5:13]
+    holds, store_sems = refs[13:19], refs[19]
+    o_ei, o_eo, o_gain_e, o_ni, o_no, o_gain_n = holds
     d_ei, d_eo, d_ni, d_no = depths
-    moves = [(edge_in, edge_hold, edge_out), (node_in, node_hold, node_out)]
-    loads = [
-        pltpu.make_async_copy(source, hold, load_sems.at[order])
-        for order, (source, hold, _) in enumerate(moves)
+    stores = [
+        pltpu.make_async_copy(source, out, store_sems.at[order])
+        for order, (source, out) in enumerate(zip((edge_in, node_in) + tuple(holds), outs))
     ]
-    for load in loads:
-        load.start()
+    stores[0].start()
+    stores[1].start()
+    for quarter in range(4):
+        span = slice(quarter * LANES, (quarter + 1) * LANES)
+        o_ei[:, span] = sum_e[quarter].astype(F32) * factor
+    stores[2].start()
     for quarter in range(4):
         span = slice(quarter * LANES, (quarter + 1) * LANES)
         o_ni[:, span] = sum_n[quarter, :d_ni].astype(F32) * factor
         o_no[:, span] = sum_n[quarter, d_ni:].astype(F32) * factor
-        o_ei[:, span] = sum_e[quarter].astype(F32) * factor
         o_eo[:, span] = sum_o[quarter, :d_eo].astype(F32) * factor
+    for order in (3, 5, 6):
+        stores[order].start()
     piece = o_gain_e.shape[1]
     p = lax.axis_index("patch")
     own = jnp.zeros((PACK, piece), F32)
@@ -480,21 +586,25 @@
         own += dot(sum_o[quarter, d_eo:], pick)
     o_gain_e[...] = own[0:1] * factor
     o_gain_n[...] = own[1:2] * factor
-    stores = []
-    for order, (_, hold, out) in enumerate(moves):
-        loads[order].wait()
-        stores.append(pltpu.make_async_copy(hold, out, store_sems.at[order]))
+    for order in (4, 7):
         stores[order].start()
     for store in stores:
         store.wait()
 
 
 def reduction_scratch(zs, depth):
+    middle = depth // 2 // PACK * PACK
+    rest = depth - middle
     shapes = (
-        (2, zs, 4, depth),
-        (zs, 4, depth),
-        (4, zs, depth),
-        (3, zs, depth),
+        (2, zs, 2, 2, depth),
+        (zs, 2, 2, depth),
+        (2, 2, zs, depth),
+        (2, zs, middle),
+        (2, zs, rest),
+        (zs, middle),
+        (zs, rest),
+        (zs, rest),
+        (zs, middle),
         (zs, depth),
         (zs - 1, depth),
         (4, depth),
@@ -572,13 +682,12 @@
         gain_node[None],
         node_cot[0],
         edge_cot[0],
-        tile_count,
+        tile_count[None],
     )
-    scratch = [pltpu.VMEM(operand.shape, operand.dtype) for operand in operands[:-1]]
-    scratch += [pltpu.SMEM(tile_count.shape, tile_count.dtype)]
+    scratch = [pltpu.VMEM(operand.shape, operand.dtype) for operand in operands]
+    if not fused:
+        scratch += [pltpu.VMEM((edges, width), BF), pltpu.VMEM((nodes, width), BF)]
     scratch += [
-        pltpu.VMEM((edges, width), BF),
-        pltpu.VMEM((nodes, width), BF),
         pltpu.SemaphoreType.DMA((len(operands),)),
         pltpu.SemaphoreType.DMA((2,)),
     ]
@@ -597,9 +706,9 @@
     if fused:
         for depth, halves in ((d_ni + d_no, 2), (d_ei, 2), (d_eo + PACK, 1)):
             reductions += reduction_scratch(zs, depth)
-            n_copies += zs + 3 * halves + zs - 1 + 3
+            n_copies += zs + 4 * halves + zs - 1 + 3
         summed_shapes = [
-            jax.ShapeDtypeStruct((4, depth, LANES), BF)
+            pltpu.VMEM((4, depth, LANES), BF)
             for depth in (d_ni + d_no, d_ei, d_eo + PACK)
         ]
     else:
@@ -609,20 +718,17 @@
     scratch += reductions
 
     vmem = pl.BlockSpec(memory_space=pltpu.VMEM)
+    big = pltpu.VMEM if fused else jax.ShapeDtypeStruct
     anywhere = pl.BlockSpec(memory_space=pl.ANY)
     sizes = (n_group, n_patch, padded, tile, senders.shape[1], fused, depths)
     edge_grad, node_grad, *sums = pl.pallas_call(
         functools.partial(kernel, sizes),
-        out_shape=[
-            jax.ShapeDtypeStruct((edges, width), BF),
-            jax.ShapeDtypeStruct((nodes, width), BF),
-        ]
-        + summed_shapes,
+        out_shape=[big((edges, width), BF), big((nodes, width), BF)] + summed_shapes,
         in_specs=[anywhere] * len(operands),
-        out_specs=[anywhere] * 2 + [vmem] * len(summed_shapes),
+        out_specs=[vmem if fused else anywhere] * 2 + [vmem] * len(summed_shapes),
         scratch_shapes=scratch,
         compiler_params=pltpu.CompilerParams(
-            collective_id=0, has_side_effects=True, vmem_limit_bytes=63 * 1024 * 1024
+            collective_id=0, has_side_effects=True, vmem_limit_bytes=54 * 1024 * 1024
         ),
     )(*operands)
     if fused:
@@ -642,16 +748,19 @@
                 o_no,
                 gain_out,
             ],
-            in_specs=[anywhere] * 2 + [vmem] * 3,
-            out_specs=[anywhere] * 2 + [vmem] * 6,
+            in_specs=[vmem] * 5,
+            out_specs=[anywhere] * 8,
             scratch_shapes=[
-                pltpu.VMEM((edges, width), BF),
-                pltpu.VMEM((nodes, width), BF),
-                pltpu.SemaphoreType.DMA((2,)),
-                pltpu.SemaphoreType.DMA((2,)),
+                pltpu.VMEM((d_ei, width), F32),
+                pltpu.VMEM((d_eo, width), F32),
+                pltpu.VMEM((1, piece), F32),
+                pltpu.VMEM((d_ni, width), F32),
+                pltpu.VMEM((d_no, width), F32),
+                pltpu.VMEM((1, piece), F32),
+                pltpu.SemaphoreType.DMA((8,)),
             ],
             compiler_params=pltpu.CompilerParams(vmem_limit_bytes=16 * 1024 * 1024),
-        )(edge_grad, node_grad, *sums)
+        )(*[pltpu.with_memory_space_constraint(x, pltpu.VMEM) for x in (edge_grad, node_grad, *sums)])
         return (
             edge_grad[None],
             node_grad[None],

time: 66.6 us -> 55.9 us (0.84)
  Pallas kernels: 59.7 us -> 54.3 us
  local copies, waits for them, and re-layouts: 5.18 us -> 0 us
    unnamed x10 -> x0, local copies, waits for them, and re-layouts: 5.18 us -> none
    pallas_call x1, Pallas kernels: 57 us -> 52.7 us  [local(): pl.pallas_call(functools.partial(kernel, sizes), out_shape=[big((edges, w...]
    pallas_call x1, Pallas kernels: 2.68 us -> 1.68 us  [local(): pl.pallas_call(functools.partial(closing, factor, depths), out_shape=[jax...]
where the time goes in v2:
time: 55.9 us; the launch traced here: 55.8 us
  Pallas kernels  54.3 us (97%)
  between operations  1.45 us (3%)
    pallas_call x1, Pallas kernels, local(): pl.pallas_call(functools.partial(kernel, sizes), out_shape=[big((edges, w...  52.7 us
    pallas_call x1, Pallas kernels, local(): pl.pallas_call(functools.partial(closing, factor, depths), out_shape=[jax...  1.68 us

profile of v2, /device:TPU:0, one launch (start us, length us, event | category | flops | bytes accessed | tf_op | source)
XLA Modules:
  0.0 55.8 jit_solution(1295642442379019114)
XLA Ops:
  1.3 52.7 %shard_map.197 = (bf16[1024,512]{1,0:T(8,128)(2,1)S(1)}, bf16[1024,512]{1,0:T(8,128)(2,1)S(1)}, bf16[4,192,128]{2,1,0:T(8,128)(2,1)S(1)}, bf16[4,192,128]{2,1,0:T(8,128)(2,1)S(1)}, bf16[4,80,128]{2,1,0:T(8,128)(2,1)S(1)}) custom-call(bf16[1024,512]{1,0:T(8,128)(2,1)} %bitcast.12, s32[1,256]{1,0:T(1,128)} %refs_1_.1, s32[8,128]{1,0:T(8,128)} %refs_2_.1, ...), custom_call_target="tpu_custom_call" | custom-call | tf_op jit(solution)/shard_map/pallas_call | solution.py:724
  54.0 1.7 %shard_map.198 = (bf16[1024,512]{1,0:T(8,128)(2,1)}, bf16[1024,512]{1,0:T(8,128)(2,1)}, f32[192,512]{1,0:T(8,128)}, f32[64,512]{1,0:T(8,128)}, f32[1,64]{1,0:T(1...) custom-call(bf16[1024,512]{1,0:T(8,128)(2,1)S(1)} %get-tuple-element.21.refs_0_, ...), custom_call_target="tpu_custom_call" | custom-call | tf_op jit(solution)/shard_map/pallas_call | solution.py:739

commit v3 on v2

--- a/solution.py
+++ b/solution.py
@@ -33,18 +33,22 @@
     return (active, squash + active * (1.0 - squash))
 
 
-def normalize(values):
+def normalize(values, live=None):
     centred = values - jnp.mean(values, axis=1, keepdims=True)
     inverse = lax.rsqrt(jnp.mean(centred * centred, axis=1, keepdims=True) + epsilon)
+    if live is not None:
+        inverse = inverse * live
     return (centred * inverse, inverse)
 
 
 def normalize_back(upstream, normed, inverse):
-    return inverse * (
+    product = upstream * normed
+    second = inverse * (
         upstream
         - jnp.mean(upstream, axis=1, keepdims=True)
-        - normed * jnp.mean(upstream * normed, axis=1, keepdims=True)
+        - normed * jnp.mean(product, axis=1, keepdims=True)
     )
+    return (second.astype(BF), jnp.sum(product, axis=0, keepdims=True))
 
 
 def hot(index, shape, axis, base):
@@ -53,22 +57,33 @@
     )
 
 
+class Waited:
+    def __init__(self, copies, copy, slot):
+        self.copies, self.copy, self.slot = copies, copy, slot
+
+    def wait(self):
+        self.copy.wait()
+        self.copies.free.append(self.slot)
+
+
 class Copies:
     def __init__(self, send_sems, recv_sems):
         self.send_sems, self.recv_sems, self.used = send_sems, recv_sems, 0
+        self.free = list(range(send_sems.shape[0]))
 
     def start(self, source, target, device):
+        slot = self.free.pop(0)
         copy = pltpu.make_async_remote_copy(
             src_ref=source,
             dst_ref=target,
-            send_sem=self.send_sems.at[self.used],
+            send_sem=self.send_sems.at[slot],
             recv_sem=self.recv_sems.at[self.used],
             device_id=device,
             device_id_type=MESH,
         )
         self.used += 1
         copy.start()
-        return copy
+        return Waited(self, copy, slot)
 
 
 def wait_all(copies):
@@ -122,56 +137,61 @@
 class Reduction:
     def __init__(self, copies, refs, place):
         self.copies, self.place = copies, place
-        self.g, self.rc, self.a, self.r1x, self.r1y, self.b0, self.b1 = refs[:7]
-        self.r2x, self.r2y, self.c, self.r3, self.f = refs[7:]
-        depth, middle = self.c.shape[1], self.r1x.shape[2]
+        self.g, self.rc, self.sx, self.sy, self.ox, self.oy = refs[:6]
+        self.r1x, self.r1y, self.b0, self.b1, self.r2x, self.r2y, self.c, self.r3, self.f = refs[6:]
+        depth, middle = self.c.shape[1], self.sx.shape[2]
         self.low, self.high = pl.ds(0, middle), pl.ds(middle, depth - middle)
-        self.pairs, self.first, self.second = [], {}, []
-
-    def put(self, k, row, size, value):
+        self.pairs, self.first, self.second = {}, {}, []
+
+    def put(self, first, last, row, size, value, skip=0):
         value = value.astype(BF)
-        for c in range(2):
-            for quarter in range(4):
-                self.g[c, k, quarter // 2, quarter % 2, row : row + size, :] = value[
-                    c * size : (c + 1) * size, quarter * LANES : (quarter + 1) * LANES
-                ]
-
-    def pair(self, k):
+        each = value.shape[0] // (2 * (last - first))
+        for k in range(first, last):
+            for c in range(2):
+                start = (2 * (k - first) + c) * each + skip
+                for quarter in range(4):
+                    self.g[c, k, quarter // 2, quarter % 2, row : row + size, :] = value[
+                        start : start + size, quarter * LANES : (quarter + 1) * LANES
+                    ]
+
+    def pair(self, first, last):
         here = self.place
-        self.pairs.append(
-            self.copies.start(self.g.at[1 - here.core, k], self.rc.at[k], here.partner)
+        span = pl.ds(first, last - first)
+        self.pairs[first] = self.copies.start(
+            self.g.at[1 - here.core, span], self.rc.at[span], here.partner
         )
+
+    def joint(self, k, gy, gx, rows):
+        own = self.g[self.place.core, k, gy, gx, rows].astype(F32)
+        return (own + self.rc[k, gy, gx, rows].astype(F32)).astype(BF)
 
     def step1(self, first, last):
         here = self.place
         for k in range(first, last):
-            self.pairs[k].wait()
-            for gy in range(2):
-                for gx in range(2):
-                    self.a[gy, gx, k] = (
-                        self.g[here.core, k, gy, gx].astype(F32) + self.rc[k, gy, gx].astype(F32)
-                    ).astype(BF)
+            if k in self.pairs:
+                self.pairs[k].wait()
+            for other in range(2):
+                self.sx[k, other] = self.joint(k, other, 1 - here.gx, self.low)
+                self.sy[k, other] = self.joint(k, 1 - here.gy, other, self.high)
         span = pl.ds(first, last - first)
         self.first[first] = [
-            self.copies.start(
-                self.a.at[:, 1 - here.gx, span, self.low], self.r1x.at[:, span], here.x_peer
-            ),
-            self.copies.start(
-                self.a.at[1 - here.gy, :, span, self.high], self.r1y.at[:, span], here.y_peer
-            ),
+            self.copies.start(self.sx.at[span], self.r1x.at[span], here.x_peer),
+            self.copies.start(self.sy.at[span], self.r1y.at[span], here.y_peer),
         ]
+        for k in range(first, last):
+            for other in range(2):
+                self.ox[k, other] = self.joint(k, other, here.gx, self.low)
+                self.oy[k, other] = self.joint(k, here.gy, other, self.high)
 
     def step2(self, first, last):
         here = self.place
         wait_all(self.first[first])
         for k in range(first, last):
             self.b0[k] = (
-                self.a[1 - here.gy, here.gx, k, self.low].astype(F32)
-                + self.r1x[1 - here.gy, k].astype(F32)
+                self.ox[k, 1 - here.gy].astype(F32) + self.r1x[k, 1 - here.gy].astype(F32)
             ).astype(BF)
             self.b1[k] = (
-                self.a[here.gy, 1 - here.gx, k, self.high].astype(F32)
-                + self.r1y[1 - here.gx, k].astype(F32)
+                self.oy[k, 1 - here.gx].astype(F32) + self.r1y[k, 1 - here.gx].astype(F32)
             ).astype(BF)
         span = pl.ds(first, last - first)
         self.second += [
@@ -184,18 +204,18 @@
         wait_all(self.second)
         for k in range(here.zs):
             self.c[k, self.low] = (
-                self.a[here.gy, here.gx, k, self.low].astype(F32)
-                + self.r1x[here.gy, k].astype(F32)
+                self.ox[k, here.gy].astype(F32)
+                + self.r1x[k, here.gy].astype(F32)
                 + self.r2y[k].astype(F32)
             ).astype(BF)
             self.c[k, self.high] = (
-                self.a[here.gy, here.gx, k, self.high].astype(F32)
-                + self.r1y[here.gx, k].astype(F32)
+                self.oy[k, here.gx].astype(F32)
+                + self.r1y[k, here.gx].astype(F32)
                 + self.r2x[k].astype(F32)
             ).astype(BF)
         self.moves = []
-        for step in range(1, here.zs):
-            there = lax.rem(here.z + step, here.zs)
+        for step in range(here.zs - 1, 0, -1):
+            there = flipped(here.z, step)
             self.moves.append(
                 self.copies.start(
                     self.c.at[there],
@@ -219,7 +239,7 @@
         out[...] = self.f[...]
 
 
-COUNT_SHARES = 12
+COUNT_SHARES = 15
 
 
 def kernel(sizes, *refs):
@@ -233,7 +253,7 @@
 
     stored = take(14)
     edge_out, node_out = take(2)
-    sums = take(3 if fused else 5)
+    sums = take(5)
     loaded = take(14)
     node, list_in, send_tiles, recv_tiles, edge, w_ei, w_eo, gain_e = loaded[:8]
     w_ni, w_no, gain_n, node_cot, edge_cot, count = loaded[8:]
@@ -243,6 +263,7 @@
     outgoing, incoming, spread, returned = take(4)
     x_s, x_r, e_first, hidden, normed, inverse, message, joined = take(8)
     n_hidden, n_first, g_second, g_first, acc, gj, ge_second, ge_first, gs, gr, gains = take(11)
+    recv_hot = take(1)[0] if fused else None
     send_sems, recv_sems = take(2)
     nodes, width = node.shape
     edges = edge.shape[0]
@@ -251,7 +272,7 @@
     gi, p = place.gi, place.p
     copies = Copies(send_sems, recv_sems)
     barrier = pltpu.get_barrier_semaphore()
-    if fused and n_patch & (n_patch - 1) == 0:
+    if fused:
         others = [flipped(p, d) for d in range(n_patch - 1, 0, -1)]
     else:
         others = [lax.rem(p + d, n_patch) for d in range(1, n_patch)]
@@ -265,8 +286,9 @@
         pltpu.make_async_copy(source, target, load_sems.at[order])
         for order, (source, target) in enumerate(zip(stored, loaded))
     ]
-    for load in loads:
-        load.start()
+    first = (1, 0, 2, 3) if fused else range(len(loads))
+    for order in first:
+        loads[order].start()
 
     def column_of(line, column):
         for order in range(column.shape[0] // LANES):
@@ -275,6 +297,9 @@
             column[span, :] = jnp.transpose(wide)[:, :1].astype(jnp.int32)
 
     loads[1].wait()
+    for order in range(len(loads)):
+        if order not in first:
+            loads[order].start()
     list_row[...] = list_in[...]
     column_of(list_row, list_col)
     loads[0].wait()
@@ -310,7 +335,10 @@
     @pl.loop(0, edges // long, unroll=fused)
     def _(k):
         rows = rows_of(k, long)
-        latent = dot(hot(recv_col[rows, :], (long, nodes), 1, 0), node[...]).astype(BF)
+        chosen = hot(recv_col[rows, :], (long, nodes), 1, 0)
+        if fused:
+            recv_hot[rows, :] = chosen
+        latent = dot(chosen, node[...]).astype(BF)
         x_r[rows, :] = latent
         e_first[rows, :] = dot(edge[rows, :], w_ei[:width, :]) + dot(latent, w_ei[2 * width :, :])
 
@@ -355,10 +383,10 @@
 
     def edge_message(k, second):
         rows = rows_of(k)
-        norm, inv = normalize(second)
+        norm, inv = normalize(second, live_of(k))
         normed[rows, :] = norm
         inverse[rows, :] = inv
-        message[rows, :] = (live_of(k) * (gain_e[...] * norm)).astype(BF)
+        message[rows, :] = (gain_e[...] * norm).astype(BF)
 
     staggered(edge_tiles, (edge_first, edge_hidden, edge_message), unrolled=fused)
 
@@ -380,30 +408,34 @@
         rows = rows_of(k)
         norm, inv = normalize(second)
         up = node_cot[rows, :].astype(F32)
-        gains[1:2, :] += jnp.sum(up * norm, axis=0, keepdims=True)
-        second = normalize_back(up * gain_n[...], norm, inv).astype(BF)
+        second, total = normalize_back(up * gain_n[...], norm, inv)
+        gains[1:2, :] += total
         g_second[rows, :] = second
         return (slope, dot_rt(second, w_no[...]))
 
     def node_back(k, held):
         slope, grad = held
-        rows = rows_of(k)
-        grad = (grad * slope).astype(BF)
-        g_first[rows, :] = grad
-        acc[rows, :] = node_cot[rows, :].astype(F32) + dot_rt(grad, w_ni[:width, :])
-        gj[rows, :] = dot_rt(grad, w_ni[width:, :]).astype(BF)
+        g_first[rows_of(k), :] = (grad * slope).astype(BF)
 
     staggered(node_tiles, (node_first, node_hidden, node_second, node_back), unrolled=fused)
 
+    def node_message():
+        @pl.loop(0, nodes // long, unroll=fused)
+        def _(k):
+            rows = rows_of(k, long)
+            gj[rows, :] = dot_rt(g_first[rows, :], w_ni[width:, :]).astype(BF)
+
     def edge_taken(k, _):
+        if fused:
+            return dot(recv_hot[rows_of(k), :], gj[...])
         return dot(hot(recv_col[rows_of(k), :], (tile, nodes), 1, 0), gj[...])
 
     def edge_second(k, taken):
         rows = rows_of(k)
         norm = normed[rows, :]
-        grad = live_of(k) * (edge_cot[rows, :].astype(F32) + taken)
-        gains[0:1, :] += jnp.sum(grad * norm, axis=0, keepdims=True)
-        second = normalize_back(grad * gain_e[...], norm, inverse[rows, :]).astype(BF)
+        grad = edge_cot[rows, :].astype(F32) + taken
+        second, total = normalize_back(grad * gain_e[...], norm, inverse[rows, :])
+        gains[0:1, :] += total
         ge_second[rows, :] = second
         return dot_rt(second, w_eo[...])
 
@@ -412,6 +444,21 @@
         ge_first[rows, :] = (grad * e_first[rows, :]).astype(BF)
 
     edge_stages = (edge_taken, edge_second, edge_back)
+    moving = []
+
+    def send_back():
+        @pl.loop(0, edges // long, unroll=fused)
+        def _(k):
+            rows = rows_of(k, long)
+            gs[rows, :] = dot_rt(ge_first[rows, :], w_ei[width : 2 * width, :]).astype(BF)
+
+        back = dot(hot(send_row[...], (halo, edges), 0, nodes), gs[...]).astype(BF)
+        spread[...] = back.reshape(n_patch, padded, width)
+        moving.extend(
+            copies.start(spread.at[other], returned.at[p], peer)
+            for other, peer in zip(others, peers)
+        )
+        returned[p] = spread[p]
 
     def rows_product(sources, start, stop, right):
         parts = []
@@ -426,75 +473,67 @@
         zs = place.zs
         half = zs // 2
         d_ei, d_eo, d_ni, d_no = depths
-        red_n = Reduction(copies, take(COUNT_SHARES), place)
-        red_e = Reduction(copies, take(COUNT_SHARES), place)
-        red_o = Reduction(copies, take(COUNT_SHARES), place)
+        red_no, red_ni, red_ea, red_eb, red_o = [
+            Reduction(copies, take(COUNT_SHARES), place) for _ in range(5)
+        ]
+        d_ea = d_ei // 2 // PACK * PACK
+        red_no.put(0, zs, 0, d_no, dot_lt(n_hidden[...], g_second[...]))
+        red_no.pair(0, zs)
         for first in (0, half):
-            for k in range(first, first + half):
-                start = 2 * k * d_ni
-                value = rows_product((node, joined), start, start + 2 * d_ni, g_first[...])
-                red_n.put(k, 0, d_ni, value)
-                value = dot_lt(n_hidden[:, 2 * k * d_no : 2 * (k + 1) * d_no], g_second[...])
-                red_n.put(k, d_ni, d_no, value)
-            for k in range(first, first + half):
-                red_n.pair(k)
-        red_n.step1(0, half)
-        staggered(edge_tiles, edge_stages, hooks={2: lambda: red_n.step1(half, zs)})
+            last = first + half
+            value = rows_product((node, joined), 2 * first * d_ni, 2 * last * d_ni, g_first[...])
+            red_ni.put(first, last, 0, d_ni, value)
+            red_ni.pair(first, last)
+            if first == 0:
+                red_no.step1(0, zs)
+        node_message()
+        red_ni.step1(0, half)
+        staggered(edge_tiles, edge_stages, hooks={2: lambda: red_ni.step1(half, zs)})
+        red_no.step2(0, zs)
+        gains[0:1, :] = gains[0:1, :] / gain_e[...]
+        gains[1:2, :] = gains[1:2, :] / gain_n[...]
+        total = gains[...].astype(BF)
+        red_o.put(0, zs, 0, d_eo, dot_lt(hidden[...], ge_second[...]))
+        red_o.put(0, zs, d_eo, PACK, jnp.concatenate([total] * (2 * zs), axis=0))
+        red_o.pair(0, zs)
+        red_ni.step2(0, half)
         for first in (0, half):
-            for k in range(first, first + half):
-                start = 2 * k * d_ei
-                value = rows_product((edge, x_s, x_r), start, start + 2 * d_ei, ge_first[...])
-                red_e.put(k, 0, d_ei, value)
-            for k in range(first, first + half):
-                red_e.pair(k)
-            if first == 0:
-                red_n.step2(0, half)
-        red_e.step1(0, half)
-        red_n.step2(half, zs)
-        total = gains[...].astype(BF)
-        total = jnp.concatenate([total, total], axis=0)
-        for k in range(zs):
-            red_o.put(
-                k, 0, d_eo, dot_lt(hidden[:, 2 * k * d_eo : 2 * (k + 1) * d_eo], ge_second[...])
+            last = first + half
+            value = rows_product(
+                (edge, x_s, x_r), 2 * first * d_ei, 2 * last * d_ei, ge_first[...]
             )
-            red_o.put(k, d_eo, PACK, total)
-        for k in range(zs):
-            red_o.pair(k)
-        red_e.step1(half, zs)
+            red_ea.put(first, last, 0, d_ea, value)
+            red_eb.put(first, last, 0, d_ei - d_ea, value, skip=d_ea)
+            red_ea.pair(first, last)
+            red_eb.pair(first, last)
+        red_o.step1(0, zs)
+        red_ni.step2(half, zs)
+        send_back()
+        red_ea.step1(0, zs)
+        red_eb.step1(0, zs)
     else:
         o_ei, o_eo, o_ni, o_no, o_gain = sums
         o_ni[:width, :] = dot_lt(node[...], g_first[...])
         o_ni[width:, :] = dot_lt(joined[...], g_first[...])
         o_no[...] = dot_lt(n_hidden[...], g_second[...])
+        node_message()
         staggered(edge_tiles, edge_stages, unrolled=False)
         o_ei[:width, :] = dot_lt(edge[...], ge_first[...])
         o_ei[width : 2 * width, :] = dot_lt(x_s[...], ge_first[...])
         o_ei[2 * width :, :] = dot_lt(x_r[...], ge_first[...])
         o_eo[...] = dot_lt(hidden[...], ge_second[...])
         o_gain[...] = gains[...]
-
-    @pl.loop(0, edges // long, unroll=fused)
-    def _(k):
-        rows = rows_of(k, long)
-        gs[rows, :] = dot_rt(ge_first[rows, :], w_ei[width : 2 * width, :]).astype(BF)
-
-    back = dot(hot(send_row[...], (halo, edges), 0, nodes), gs[...]).astype(BF)
-    spread[...] = back.reshape(n_patch, padded, width)
-    moving = [
-        copies.start(spread.at[other], returned.at[p], peer)
-        for other, peer in zip(others, peers)
-    ]
-    returned[p] = spread[p]
-    if fused:
-        red_o.step1(0, zs)
+        o_gain[0:1, :] = gains[0:1, :] / gain_e[...]
+        o_gain[1:2, :] = gains[1:2, :] / gain_n[...]
+
+    if not fused:
+        send_back()
 
     @pl.loop(0, edges // long, unroll=fused)
     def _(k):
         rows = rows_of(k, long)
         gr[rows, :] = dot_rt(ge_first[rows, :], w_ei[2 * width :, :]).astype(BF)
 
-    if fused:
-        red_n.along()
 
     @pl.loop(0, edges // long, unroll=fused)
     def _(k):
@@ -511,22 +550,28 @@
 
     def gather_back(k):
         rows = rows_of(k, long)
-        acc[rows, :] += dot(hot(send_row[...], (long, edges), 0, k * long), gs[...]) + dot(
-            hot(recv_row[...], (long, edges), 0, k * long), gr[...]
+        acc[rows, :] = (
+            node_cot[rows, :].astype(F32)
+            + dot_rt(g_first[rows, :], w_ni[:width, :])
+            + dot(hot(send_row[...], (long, edges), 0, k * long), gs[...])
+            + dot(hot(recv_row[...], (long, edges), 0, k * long), gr[...])
         )
 
-    if fused:
-        red_e.step2(0, half)
     gathers = nodes // long
     pl.loop(0, gathers // 2, unroll=fused)(gather_back)
     if fused:
-        red_e.step2(half, zs)
         red_o.step2(0, zs)
+        red_no.along()
+        red_ni.along()
     pl.loop(gathers // 2, gathers, unroll=fused)(gather_back)
     if fused:
-        red_e.along()
+        red_ea.step2(0, zs)
+        red_eb.step2(0, zs)
         red_o.along()
-        red_n.share()
+        red_ea.along()
+        red_eb.along()
+        red_no.share()
+        red_ni.share()
     wait_all(moving)
 
     @pl.loop(0, node_tiles, unroll=fused)
@@ -544,19 +589,22 @@
         stores.append(pltpu.make_async_copy(node_grad, node_out, store_sems.at[1]))
         stores[1].start()
     if fused:
-        red_e.share()
         red_o.share()
-        red_n.finish(sums[0])
-        red_e.finish(sums[1])
-        red_o.finish(sums[2])
+        red_ea.share()
+        red_eb.share()
+        red_no.finish(sums[0])
+        red_ni.finish(sums[1])
+        red_o.finish(sums[4])
+        red_ea.finish(sums[2])
+        red_eb.finish(sums[3])
     for store in stores:
         store.wait()
 
 
 def closing(factor, depths, *refs):
-    edge_in, node_in, sum_n, sum_e, sum_o = refs[:5]
-    outs = refs[5:13]
-    holds, store_sems = refs[13:19], refs[19]
+    edge_in, node_in, sum_no, sum_ni, sum_ea, sum_eb, sum_o = refs[:7]
+    outs = refs[7:15]
+    holds, store_sems = refs[15:21], refs[21]
     o_ei, o_eo, o_gain_e, o_ni, o_no, o_gain_n = holds
     d_ei, d_eo, d_ni, d_no = depths
     stores = [
@@ -567,12 +615,13 @@
     stores[1].start()
     for quarter in range(4):
         span = slice(quarter * LANES, (quarter + 1) * LANES)
-        o_ei[:, span] = sum_e[quarter].astype(F32) * factor
+        o_ei[: sum_ea.shape[1], span] = sum_ea[quarter].astype(F32) * factor
+        o_ei[sum_ea.shape[1] :, span] = sum_eb[quarter].astype(F32) * factor
     stores[2].start()
     for quarter in range(4):
         span = slice(quarter * LANES, (quarter + 1) * LANES)
-        o_ni[:, span] = sum_n[quarter, :d_ni].astype(F32) * factor
-        o_no[:, span] = sum_n[quarter, d_ni:].astype(F32) * factor
+        o_ni[:, span] = sum_ni[quarter].astype(F32) * factor
+        o_no[:, span] = sum_no[quarter].astype(F32) * factor
         o_eo[:, span] = sum_o[quarter, :d_eo].astype(F32) * factor
     for order in (3, 5, 6):
         stores[order].start()
@@ -598,9 +647,12 @@
     shapes = (
         (2, zs, 2, 2, depth),
         (zs, 2, 2, depth),
-        (2, 2, zs, depth),
-        (2, zs, middle),
-        (2, zs, rest),
+        (zs, 2, middle),
+        (zs, 2, rest),
+        (zs, 2, middle),
+        (zs, 2, rest),
+        (zs, 2, middle),
+        (zs, 2, rest),
         (zs, middle),
         (zs, rest),
         (zs, rest),
@@ -665,8 +717,10 @@
     fused = (
         n_group == 4
         and n_patch % 4 == 0
+        and n_patch & (n_patch - 1) == 0
         and width == 4 * LANES
         and all(d % PACK == 0 and 2 * d % LANES == 0 for d in depths)
+        and depths[0] >= 2 * PACK
     )
     operands = (
         node_tape[0],
@@ -700,21 +754,23 @@
     scratch += [by_edge, by_node]
     scratch += [by_node, wide_node, by_node, by_node, wide_node, by_node]
     scratch += [by_edge, by_edge, by_edge, by_edge, pltpu.VMEM((PACK, width), F32)]
+    if fused:
+        scratch += [pltpu.VMEM((edges, nodes), BF)]
     n_copies = 2 * (n_patch - 1)
     d_ei, d_eo, d_ni, d_no = depths
     reductions = []
     if fused:
-        for depth, halves in ((d_ni + d_no, 2), (d_ei, 2), (d_eo + PACK, 1)):
+        d_ea = d_ei // 2 // PACK * PACK
+        shared = (d_no, d_ni, d_ea, d_ei - d_ea, d_eo + PACK)
+        for depth, pairs, halves in zip(shared, (1, 2, 2, 2, 1), (1, 2, 1, 1, 1)):
             reductions += reduction_scratch(zs, depth)
-            n_copies += zs + 4 * halves + zs - 1 + 3
-        summed_shapes = [
-            pltpu.VMEM((4, depth, LANES), BF)
-            for depth in (d_ni + d_no, d_ei, d_eo + PACK)
-        ]
+            n_copies += pairs + 4 * halves + zs - 1 + 3
+        summed_shapes = [pltpu.VMEM((4, depth, LANES), BF) for depth in shared]
     else:
         summed_shapes = [jax.ShapeDtypeStruct((w.shape[0], width), F32) for w in weights]
         summed_shapes += [jax.ShapeDtypeStruct((PACK, width), F32)]
-    scratch += [pltpu.SemaphoreType.DMA((n_copies,)), pltpu.SemaphoreType.DMA((n_copies,))]
+    in_flight = n_copies // 2 + 4 if fused else n_copies
+    scratch += [pltpu.SemaphoreType.DMA((in_flight,)), pltpu.SemaphoreType.DMA((n_copies,))]
     scratch += reductions
 
     vmem = pl.BlockSpec(memory_space=pltpu.VMEM)
@@ -748,7 +804,7 @@
                 o_no,
                 gain_out,
             ],
-            in_specs=[vmem] * 5,
+            in_specs=[vmem] * 7,
             out_specs=[anywhere] * 8,
             scratch_shapes=[
                 pltpu.VMEM((d_ei, width), F32),

time: 55.9 us -> 55 us (0.984)
  Pallas kernels: 54.3 us -> 53.4 us
    pallas_call x1, Pallas kernels: 52.7 us -> 51.7 us  [local(): pl.pallas_call(functools.partial(kernel, sizes), out_shape=[big((edges, w...]
where the time goes in v3:
time: 55 us; the launch traced here: 54.8 us
  Pallas kernels  53.4 us (97%)
  between operations  1.45 us (3%)
    pallas_call x1, Pallas kernels, local(): pl.pallas_call(functools.partial(kernel, sizes), out_shape=[big((edges, w...  51.7 us
    pallas_call x1, Pallas kernels, local(): pl.pallas_call(functools.partial(closing, factor, depths), out_shape=[jax...  1.68 us

profile of v3, /device:TPU:0, one launch (start us, length us, event | category | flops | bytes accessed | tf_op | source)
XLA Modules:
  0.0 54.8 jit_solution(6058605978130832141)
XLA Ops:
  1.3 51.7 %shard_map.197 = (bf16[1024,512]{1,0:T(8,128)(2,1)S(1)}, bf16[1024,512]{1,0:T(8,128)(2,1)S(1)}, bf16[4,64,128]{2,1,0:T(8,128)(2,1)S(1)}, bf16[4,128,128]{2,1,0:T...) custom-call(bf16[1024,512]{1,0:T(8,128)(2,1)} %bitcast.12, ...), custom_call_target="tpu_custom_call" | custom-call | tf_op jit(solution)/shard_map/pallas_call | solution.py:780
  53.0 1.7 %shard_map.198 = (bf16[1024,512]{1,0:T(8,128)(2,1)}, bf16[1024,512]{1,0:T(8,128)(2,1)}, f32[192,512]{1,0:T(8,128)}, f32[64,512]{1,0:T(8,128)}, f32[1,64]{1,0:T(1...) custom-call(bf16[1024,512]{1,0:T(8,128)(2,1)S(1)} %get-tuple-element.23.refs_0_, ...), custom_call_target="tpu_custom_call" | custom-call | tf_op jit(solution)/shard_map/pallas_call | solution.py:795

commit v4 on v3

--- a/solution.py
+++ b/solution.py
@@ -239,6 +239,50 @@
         out[...] = self.f[...]
 
 
+class GainSum:
+    def __init__(self, copies, refs, place):
+        self.copies, self.place = copies, place
+        self.own, self.got = refs
+
+    def send(self, order, first, devices):
+        self.order, self.first = order, first
+        self.moves = [
+            self.copies.start(self.own.at[order], self.got.at[first + slot], device)
+            for slot, device in enumerate(devices)
+        ]
+
+    def gather(self):
+        wait_all(self.moves)
+        total = self.own[self.order]
+        for slot in range(len(self.moves)):
+            total += self.got[self.first + slot]
+        return total
+
+    def start(self, gains):
+        for row in range(2):
+            for quarter in range(4):
+                line = 4 * row + quarter
+                self.own[0, line : line + 1, :] = gains[
+                    row : row + 1, quarter * LANES : (quarter + 1) * LANES
+                ]
+        self.send(0, 0, [self.place.partner])
+
+    def members(self):
+        self.own[1] = self.gather()
+        self.send(1, 1, self.place.members)
+
+    def along(self):
+        here = self.place
+        self.own[2] = self.gather()
+        chips = [flipped(here.z, step) for step in range(1, here.zs)]
+        self.send(
+            2, 4, [{"group": here.gi, "patch": chip * 2 + here.core} for chip in chips]
+        )
+
+    def finish(self, out):
+        out[...] = self.gather()
+
+
 COUNT_SHARES = 15
 
 
@@ -253,7 +297,7 @@
 
     stored = take(14)
     edge_out, node_out = take(2)
-    sums = take(5)
+    sums = take(6 if fused else 5)
     loaded = take(14)
     node, list_in, send_tiles, recv_tiles, edge, w_ei, w_eo, gain_e = loaded[:8]
     w_ni, w_no, gain_n, node_cot, edge_cot, count = loaded[8:]
@@ -330,7 +374,7 @@
 
     long = 2 * tile if fused and edges % (2 * tile) == 0 and nodes % (2 * tile) == 0 else tile
 
-    edge_tiles, node_tiles = edges // tile, nodes // tile
+    edge_tiles = edges // tile
 
     @pl.loop(0, edges // long, unroll=fused)
     def _(k):
@@ -391,13 +435,13 @@
     staggered(edge_tiles, (edge_first, edge_hidden, edge_message), unrolled=fused)
 
     def node_first(k, _):
-        rows = rows_of(k)
-        got = dot(hot(recv_row[...], (tile, edges), 0, k * tile), message[...]).astype(BF)
+        rows = rows_of(k, long)
+        got = dot(hot(recv_row[...], (long, edges), 0, k * long), message[...]).astype(BF)
         joined[rows, :] = got
         return n_first[rows, :] + dot(got, w_ni[width:, :])
 
     def node_hidden(k, first):
-        rows = rows_of(k)
+        rows = rows_of(k, long)
         active, slope = silu_pair(first)
         hid = active.astype(BF)
         n_hidden[rows, :] = hid
@@ -405,7 +449,7 @@
 
     def node_second(k, held):
         slope, second = held
-        rows = rows_of(k)
+        rows = rows_of(k, long)
         norm, inv = normalize(second)
         up = node_cot[rows, :].astype(F32)
         second, total = normalize_back(up * gain_n[...], norm, inv)
@@ -415,9 +459,9 @@
 
     def node_back(k, held):
         slope, grad = held
-        g_first[rows_of(k), :] = (grad * slope).astype(BF)
-
-    staggered(node_tiles, (node_first, node_hidden, node_second, node_back), unrolled=fused)
+        g_first[rows_of(k, long), :] = (grad * slope).astype(BF)
+
+    staggered(nodes // long, (node_first, node_hidden, node_second, node_back), unrolled=fused)
 
     def node_message():
         @pl.loop(0, nodes // long, unroll=fused)
@@ -446,13 +490,15 @@
     edge_stages = (edge_taken, edge_second, edge_back)
     moving = []
 
-    def send_back():
+    def send_rows_back():
         @pl.loop(0, edges // long, unroll=fused)
         def _(k):
             rows = rows_of(k, long)
             gs[rows, :] = dot_rt(ge_first[rows, :], w_ei[width : 2 * width, :]).astype(BF)
 
-        back = dot(hot(send_row[...], (halo, edges), 0, nodes), gs[...]).astype(BF)
+    def send_back():
+        back = dot(hot(send_row[...], (halo, edges), 0, nodes), ge_first[...]).astype(BF)
+        back = dot_rt(back, w_ei[width : 2 * width, :]).astype(BF)
         spread[...] = back.reshape(n_patch, padded, width)
         moving.extend(
             copies.start(spread.at[other], returned.at[p], peer)
@@ -476,6 +522,7 @@
         red_no, red_ni, red_ea, red_eb, red_o = [
             Reduction(copies, take(COUNT_SHARES), place) for _ in range(5)
         ]
+        gain_sum = GainSum(copies, take(2), place)
         d_ea = d_ei // 2 // PACK * PACK
         red_no.put(0, zs, 0, d_no, dot_lt(n_hidden[...], g_second[...]))
         red_no.pair(0, zs)
@@ -489,12 +536,12 @@
         node_message()
         red_ni.step1(0, half)
         staggered(edge_tiles, edge_stages, hooks={2: lambda: red_ni.step1(half, zs)})
+        send_back()
         red_no.step2(0, zs)
         gains[0:1, :] = gains[0:1, :] / gain_e[...]
         gains[1:2, :] = gains[1:2, :] / gain_n[...]
-        total = gains[...].astype(BF)
+        gain_sum.start(gains)
         red_o.put(0, zs, 0, d_eo, dot_lt(hidden[...], ge_second[...]))
-        red_o.put(0, zs, d_eo, PACK, jnp.concatenate([total] * (2 * zs), axis=0))
         red_o.pair(0, zs)
         red_ni.step2(0, half)
         for first in (0, half):
@@ -506,9 +553,11 @@
             red_eb.put(first, last, 0, d_ei - d_ea, value, skip=d_ea)
             red_ea.pair(first, last)
             red_eb.pair(first, last)
-        red_o.step1(0, zs)
+            if first == 0:
+                red_o.step1(0, zs)
+                gain_sum.members()
         red_ni.step2(half, zs)
-        send_back()
+        send_rows_back()
         red_ea.step1(0, zs)
         red_eb.step1(0, zs)
     else:
@@ -528,6 +577,7 @@
 
     if not fused:
         send_back()
+        send_rows_back()
 
     @pl.loop(0, edges // long, unroll=fused)
     def _(k):
@@ -558,14 +608,16 @@
         )
 
     gathers = nodes // long
+    if fused:
+        red_no.along()
+        red_ni.along()
+        red_o.step2(0, zs)
+        gain_sum.along()
     pl.loop(0, gathers // 2, unroll=fused)(gather_back)
     if fused:
-        red_o.step2(0, zs)
-        red_no.along()
-        red_ni.along()
+        red_ea.step2(0, zs)
     pl.loop(gathers // 2, gathers, unroll=fused)(gather_back)
     if fused:
-        red_ea.step2(0, zs)
         red_eb.step2(0, zs)
         red_o.along()
         red_ea.along()
@@ -574,7 +626,7 @@
         red_ni.share()
     wait_all(moving)
 
-    @pl.loop(0, node_tiles, unroll=fused)
+    @pl.loop(0, nodes // tile, unroll=fused)
     def _(k):
         rows = rows_of(k)
         node_grad[rows, :] = (
@@ -595,6 +647,7 @@
         red_no.finish(sums[0])
         red_ni.finish(sums[1])
         red_o.finish(sums[4])
+        gain_sum.finish(sums[5])
         red_ea.finish(sums[2])
         red_eb.finish(sums[3])
     for store in stores:
@@ -602,9 +655,9 @@
 
 
 def closing(factor, depths, *refs):
-    edge_in, node_in, sum_no, sum_ni, sum_ea, sum_eb, sum_o = refs[:7]
-    outs = refs[7:15]
-    holds, store_sems = refs[15:21], refs[21]
+    edge_in, node_in, sum_no, sum_ni, sum_ea, sum_eb, sum_o, sum_gain = refs[:8]
+    outs = refs[8:16]
+    holds, store_sems = refs[16:22], refs[22]
     o_ei, o_eo, o_gain_e, o_ni, o_no, o_gain_n = holds
     d_ei, d_eo, d_ni, d_no = depths
     stores = [
@@ -622,19 +675,18 @@
         span = slice(quarter * LANES, (quarter + 1) * LANES)
         o_ni[:, span] = sum_ni[quarter].astype(F32) * factor
         o_no[:, span] = sum_no[quarter].astype(F32) * factor
-        o_eo[:, span] = sum_o[quarter, :d_eo].astype(F32) * factor
+        o_eo[:, span] = sum_o[quarter].astype(F32) * factor
     for order in (3, 5, 6):
         stores[order].start()
     piece = o_gain_e.shape[1]
     p = lax.axis_index("patch")
-    own = jnp.zeros((PACK, piece), F32)
-    for quarter in range(4):
-        lane = lax.broadcasted_iota(jnp.int32, (LANES, piece), 0) + quarter * LANES
-        want = lax.broadcasted_iota(jnp.int32, (LANES, piece), 1) + p * piece
-        pick = jnp.where(lane == want, 1.0, 0.0).astype(BF)
-        own += dot(sum_o[quarter, d_eo:], pick)
-    o_gain_e[...] = own[0:1] * factor
-    o_gain_n[...] = own[1:2] * factor
+    share = LANES // piece
+    for row, hold in ((0, o_gain_e), (4, o_gain_n)):
+        line = sum_gain[pl.ds(row + lax.div(p, share), 1), :]
+        own = jnp.zeros((1, piece), F32)
+        for part in range(share):
+            own += jnp.where(lax.rem(p, share) == part, line[:, part * piece : (part + 1) * piece], 0.0)
+        hold[...] = own * factor
     for order in (4, 7):
         stores[order].start()
     for store in stores:
@@ -720,7 +772,8 @@
         and n_patch & (n_patch - 1) == 0
         and width == 4 * LANES
         and all(d % PACK == 0 and 2 * d % LANES == 0 for d in depths)
-        and depths[0] >= 2 * PACK
+        and min(depths) >= 2 * PACK
+        and LANES * n_patch % width == 0
     )
     operands = (
         node_tape[0],
@@ -761,11 +814,14 @@
     reductions = []
     if fused:
         d_ea = d_ei // 2 // PACK * PACK
-        shared = (d_no, d_ni, d_ea, d_ei - d_ea, d_eo + PACK)
+        shared = (d_no, d_ni, d_ea, d_ei - d_ea, d_eo)
         for depth, pairs, halves in zip(shared, (1, 2, 2, 2, 1), (1, 2, 1, 1, 1)):
             reductions += reduction_scratch(zs, depth)
             n_copies += pairs + 4 * halves + zs - 1 + 3
+        reductions += [pltpu.VMEM((3, 8, LANES), F32), pltpu.VMEM((3 + zs, 8, LANES), F32)]
+        n_copies += 3 + zs
         summed_shapes = [pltpu.VMEM((4, depth, LANES), BF) for depth in shared]
+        summed_shapes += [pltpu.VMEM((8, LANES), F32)]
     else:
         summed_shapes = [jax.ShapeDtypeStruct((w.shape[0], width), F32) for w in weights]
         summed_shapes += [jax.ShapeDtypeStruct((PACK, width), F32)]
@@ -804,7 +860,7 @@
                 o_no,
                 gain_out,
             ],
-            in_specs=[vmem] * 7,
+            in_specs=[vmem] * 8,
             out_specs=[anywhere] * 8,
             scratch_shapes=[
                 pltpu.VMEM((d_ei, width), F32),

time: 55 us -> 52.7 us (0.958)
  Pallas kernels: 53.4 us -> 51.1 us
    pallas_call x1, Pallas kernels: 51.7 us -> 49.4 us  [local(): pl.pallas_call(functools.partial(kernel, sizes), out_shape=[big((edges, w...]
where the time goes in v4:
time: 52.7 us; the launch traced here: 52.5 us
  Pallas kernels  51.1 us (97%)
  between operations  1.45 us (3%)
    pallas_call x1, Pallas kernels, local(): pl.pallas_call(functools.partial(kernel, sizes), out_shape=[big((edges, w...  49.4 us
    pallas_call x1, Pallas kernels, local(): pl.pallas_call(functools.partial(closing, factor, depths), out_shape=[jax...  1.69 us

profile of v4, /device:TPU:0, one launch (start us, length us, event | category | flops | bytes accessed | tf_op | source)
XLA Modules:
  0.0 52.5 jit_solution(17924984288130290048)
XLA Ops:
  1.3 49.4 %shard_map.197 = (bf16[1024,512]{1,0:T(8,128)(2,1)S(1)}, bf16[1024,512]{1,0:T(8,128)(2,1)S(1)}, bf16[4,64,128]{2,1,0:T(8,128)(2,1)S(1)}, bf16[4,128,128]{2,1,0:T...) custom-call(bf16[1024,512]{1,0:T(8,128)(2,1)} %bitcast.12, ...), custom_call_target="tpu_custom_call" | custom-call | tf_op jit(solution)/shard_map/pallas_call | solution.py:836
  50.7 1.7 %shard_map.198 = (bf16[1024,512]{1,0:T(8,128)(2,1)}, bf16[1024,512]{1,0:T(8,128)(2,1)}, f32[192,512]{1,0:T(8,128)}, f32[64,512]{1,0:T(8,128)}, f32[1,64]{1,0:T(1...) custom-call(bf16[1024,512]{1,0:T(8,128)(2,1)S(1)} %get-tuple-element.24.refs_0_, ...), custom_call_target="tpu_custom_call" | custom-call | tf_op jit(solution)/shard_map/pallas_call | solution.py:851

commit v5 on v4

--- a/solution.py
+++ b/solution.py
@@ -12,6 +12,7 @@
 F32 = jnp.float32
 LANES = 128
 PACK = 16
+PARTS = 3
 MESH = pl.DeviceIdType.MESH
 
 
@@ -69,10 +70,10 @@
 class Copies:
     def __init__(self, send_sems, recv_sems):
         self.send_sems, self.recv_sems, self.used = send_sems, recv_sems, 0
-        self.free = list(range(send_sems.shape[0]))
+        self.free = list(range(send_sems.shape[0]))[::-1]
 
     def start(self, source, target, device):
-        slot = self.free.pop(0)
+        slot = self.free.pop()
         copy = pltpu.make_async_remote_copy(
             src_ref=source,
             dst_ref=target,
@@ -109,6 +110,11 @@
                 held[k] = stages[order](k, held.get(k))
         if hooks and step in hooks:
             hooks[step]()
+
+
+def parts_of(depth):
+    each = -(-depth // PARTS // PACK) * PACK
+    return [min(each, depth - start) for start in range(0, depth, each)]
 
 
 def flipped(index, bits):
@@ -297,7 +303,7 @@
 
     stored = take(14)
     edge_out, node_out = take(2)
-    sums = take(6 if fused else 5)
+    sums = take(4 + len(parts_of(depths[0])) if fused else 5)
     loaded = take(14)
     node, list_in, send_tiles, recv_tiles, edge, w_ei, w_eo, gain_e = loaded[:8]
     w_ni, w_no, gain_n, node_cot, edge_cot, count = loaded[8:]
@@ -307,7 +313,7 @@
     outgoing, incoming, spread, returned = take(4)
     x_s, x_r, e_first, hidden, normed, inverse, message, joined = take(8)
     n_hidden, n_first, g_second, g_first, acc, gj, ge_second, ge_first, gs, gr, gains = take(11)
-    recv_hot = take(1)[0] if fused else None
+    recv_hot, recv_turned, send_hot = take(3) if fused else [None] * 3
     send_sems, recv_sems = take(2)
     nodes, width = node.shape
     edges = edge.shape[0]
@@ -399,6 +405,22 @@
         rows = rows_of(k, long)
         n_first[rows, :] = dot(node[rows, :], w_ni[:width, :])
 
+    def recv_rows(k):
+        if fused:
+            return recv_turned[rows_of(k, long), :]
+        return hot(recv_row[...], (long, edges), 0, k * long)
+
+    def send_halo(k):
+        if fused:
+            return send_hot[rows_of(k), :]
+        return hot(send_col[rows_of(k), :], (tile, halo), 1, nodes)
+
+    if fused:
+        for k in range(nodes // long):
+            recv_turned[rows_of(k, long), :] = hot(recv_row[...], (long, edges), 0, k * long)
+        for k in range(edge_tiles):
+            rows = rows_of(k)
+            send_hot[rows, :] = hot(send_col[rows, :], (tile, halo), 1, nodes)
     for load in loads[6:8] + loads[9:]:
         load.wait()
     wait_all(moving)
@@ -410,9 +432,7 @@
 
     def edge_first(k, _):
         rows = rows_of(k)
-        latent = dot(
-            hot(send_col[rows, :], (tile, halo), 1, nodes), incoming[...].reshape(halo, width)
-        )
+        latent = dot(send_halo(k), incoming[...].reshape(halo, width))
         latent = x_s[rows, :] + latent.astype(BF)
         x_s[rows, :] = latent
         return e_first[rows, :] + dot(latent, w_ei[width : 2 * width, :])
@@ -436,7 +456,7 @@
 
     def node_first(k, _):
         rows = rows_of(k, long)
-        got = dot(hot(recv_row[...], (long, edges), 0, k * long), message[...]).astype(BF)
+        got = dot(recv_rows(k), message[...]).astype(BF)
         joined[rows, :] = got
         return n_first[rows, :] + dot(got, w_ni[width:, :])
 
@@ -519,11 +539,11 @@
         zs = place.zs
         half = zs // 2
         d_ei, d_eo, d_ni, d_no = depths
-        red_no, red_ni, red_ea, red_eb, red_o = [
-            Reduction(copies, take(COUNT_SHARES), place) for _ in range(5)
+        e_depths = parts_of(d_ei)
+        red_no, red_ni, red_o, *red_e = [
+            Reduction(copies, take(COUNT_SHARES), place) for _ in range(3 + len(e_depths))
         ]
         gain_sum = GainSum(copies, take(2), place)
-        d_ea = d_ei // 2 // PACK * PACK
         red_no.put(0, zs, 0, d_no, dot_lt(n_hidden[...], g_second[...]))
         red_no.pair(0, zs)
         for first in (0, half):
@@ -532,8 +552,8 @@
             red_ni.put(first, last, 0, d_ni, value)
             red_ni.pair(first, last)
             if first == 0:
+                node_message()
                 red_no.step1(0, zs)
-        node_message()
         red_ni.step1(0, half)
         staggered(edge_tiles, edge_stages, hooks={2: lambda: red_ni.step1(half, zs)})
         send_back()
@@ -549,17 +569,19 @@
             value = rows_product(
                 (edge, x_s, x_r), 2 * first * d_ei, 2 * last * d_ei, ge_first[...]
             )
-            red_ea.put(first, last, 0, d_ea, value)
-            red_eb.put(first, last, 0, d_ei - d_ea, value, skip=d_ea)
-            red_ea.pair(first, last)
-            red_eb.pair(first, last)
+            skip = 0
+            for red, depth in zip(red_e, e_depths):
+                red.put(first, last, 0, depth, value, skip=skip)
+                skip += depth
+            for red in red_e:
+                red.pair(first, last)
             if first == 0:
                 red_o.step1(0, zs)
                 gain_sum.members()
         red_ni.step2(half, zs)
         send_rows_back()
-        red_ea.step1(0, zs)
-        red_eb.step1(0, zs)
+        for red in red_e:
+            red.step1(0, zs)
     else:
         o_ei, o_eo, o_ni, o_no, o_gain = sums
         o_ni[:width, :] = dot_lt(node[...], g_first[...])
@@ -604,7 +626,7 @@
             node_cot[rows, :].astype(F32)
             + dot_rt(g_first[rows, :], w_ni[:width, :])
             + dot(hot(send_row[...], (long, edges), 0, k * long), gs[...])
-            + dot(hot(recv_row[...], (long, edges), 0, k * long), gr[...])
+            + dot(recv_rows(k), gr[...])
         )
 
     gathers = nodes // long
@@ -615,13 +637,14 @@
         gain_sum.along()
     pl.loop(0, gathers // 2, unroll=fused)(gather_back)
     if fused:
-        red_ea.step2(0, zs)
+        red_e[0].step2(0, zs)
     pl.loop(gathers // 2, gathers, unroll=fused)(gather_back)
     if fused:
-        red_eb.step2(0, zs)
+        for red in red_e[1:]:
+            red.step2(0, zs)
         red_o.along()
-        red_ea.along()
-        red_eb.along()
+        for red in red_e:
+            red.along()
         red_no.share()
         red_ni.share()
     wait_all(moving)
@@ -642,22 +665,23 @@
         stores[1].start()
     if fused:
         red_o.share()
-        red_ea.share()
-        red_eb.share()
+        for red in red_e:
+            red.share()
         red_no.finish(sums[0])
         red_ni.finish(sums[1])
-        red_o.finish(sums[4])
-        gain_sum.finish(sums[5])
-        red_ea.finish(sums[2])
-        red_eb.finish(sums[3])
+        red_o.finish(sums[2])
+        gain_sum.finish(sums[3])
+        for red, out in zip(red_e, sums[4:]):
+            red.finish(out)
     for store in stores:
         store.wait()
 
 
 def closing(factor, depths, *refs):
-    edge_in, node_in, sum_no, sum_ni, sum_ea, sum_eb, sum_o, sum_gain = refs[:8]
-    outs = refs[8:16]
-    holds, store_sems = refs[16:22], refs[22]
+    refs = list(refs)
+    edge_in, node_in, sum_no, sum_ni, sum_o, sum_gain = refs[:6]
+    outs, holds, store_sems = refs[-15:-7], refs[-7:-1], refs[-1]
+    sum_e = refs[6:-15]
     o_ei, o_eo, o_gain_e, o_ni, o_no, o_gain_n = holds
     d_ei, d_eo, d_ni, d_no = depths
     stores = [
@@ -668,8 +692,10 @@
     stores[1].start()
     for quarter in range(4):
         span = slice(quarter * LANES, (quarter + 1) * LANES)
-        o_ei[: sum_ea.shape[1], span] = sum_ea[quarter].astype(F32) * factor
-        o_ei[sum_ea.shape[1] :, span] = sum_eb[quarter].astype(F32) * factor
+        row = 0
+        for part in sum_e:
+            o_ei[row : row + part.shape[1], span] = part[quarter].astype(F32) * factor
+            row += part.shape[1]
     stores[2].start()
     for quarter in range(4):
         span = slice(quarter * LANES, (quarter + 1) * LANES)
@@ -808,24 +834,25 @@
     scratch += [by_node, wide_node, by_node, by_node, wide_node, by_node]
     scratch += [by_edge, by_edge, by_edge, by_edge, pltpu.VMEM((PACK, width), F32)]
     if fused:
-        scratch += [pltpu.VMEM((edges, nodes), BF)]
+        scratch += [pltpu.VMEM(shape, BF) for shape in ((edges, nodes), (nodes, edges), (edges, halo))]
     n_copies = 2 * (n_patch - 1)
     d_ei, d_eo, d_ni, d_no = depths
     reductions = []
     if fused:
-        d_ea = d_ei // 2 // PACK * PACK
-        shared = (d_no, d_ni, d_ea, d_ei - d_ea, d_eo)
-        for depth, pairs, halves in zip(shared, (1, 2, 2, 2, 1), (1, 2, 1, 1, 1)):
+        e_depths = parts_of(d_ei)
+        shared = [d_no, d_ni, d_eo] + e_depths
+        pairs, halves = [1, 2, 1] + [2] * len(e_depths), [1, 2, 1] + [1] * len(e_depths)
+        for depth, pair, half in zip(shared, pairs, halves):
             reductions += reduction_scratch(zs, depth)
-            n_copies += pairs + 4 * halves + zs - 1 + 3
+            n_copies += pair + 4 * half + zs - 1 + 3
         reductions += [pltpu.VMEM((3, 8, LANES), F32), pltpu.VMEM((3 + zs, 8, LANES), F32)]
         n_copies += 3 + zs
         summed_shapes = [pltpu.VMEM((4, depth, LANES), BF) for depth in shared]
-        summed_shapes += [pltpu.VMEM((8, LANES), F32)]
+        summed_shapes.insert(3, pltpu.VMEM((8, LANES), F32))
     else:
         summed_shapes = [jax.ShapeDtypeStruct((w.shape[0], width), F32) for w in weights]
         summed_shapes += [jax.ShapeDtypeStruct((PACK, width), F32)]
-    in_flight = n_copies // 2 + 4 if fused else n_copies
+    in_flight = n_copies // 3 + 1 if fused else n_copies
     scratch += [pltpu.SemaphoreType.DMA((in_flight,)), pltpu.SemaphoreType.DMA((n_copies,))]
     scratch += reductions
 
@@ -860,7 +887,7 @@
                 o_no,
                 gain_out,
             ],
-            in_specs=[vmem] * 8,
+            in_specs=[vmem] * (2 + len(sums)),
             out_specs=[anywhere] * 8,
             scratch_shapes=[
                 pltpu.VMEM((d_ei, width), F32),

time: 52.7 us -> 52.7 us (level)
  no operation moved by 1% of the time
where the time goes in v5:
time: 52.7 us; the launch traced here: 52.5 us
  Pallas kernels  51.1 us (97%)
  between operations  1.45 us (3%)
    pallas_call x1, Pallas kernels, local(): pl.pallas_call(functools.partial(kernel, sizes), out_shape=[big((edges, w...  49.4 us
    pallas_call x1, Pallas kernels, local(): pl.pallas_call(functools.partial(closing, factor, depths), out_shape=[jax...  1.69 us

profile of v5, /device:TPU:0, one launch (start us, length us, event | category | flops | bytes accessed | tf_op | source)
XLA Modules:
  0.0 52.5 jit_solution(12717026577911052139)
XLA Ops:
  1.3 49.4 %shard_map.197 = (bf16[1024,512]{1,0:T(8,128)(2,1)S(1)}, bf16[1024,512]{1,0:T(8,128)(2,1)S(1)}, bf16[4,64,128]{2,1,0:T(8,128)(2,1)S(1)}, bf16[4,128,128]{2,1,0:T...) custom-call(bf16[1024,512]{1,0:T(8,128)(2,1)} %bitcast.12, ...), custom_call_target="tpu_custom_call" | custom-call | tf_op jit(solution)/shard_map/pallas_call | solution.py:863
  50.7 1.7 %shard_map.198 = (bf16[1024,512]{1,0:T(8,128)(2,1)}, bf16[1024,512]{1,0:T(8,128)(2,1)}, f32[192,512]{1,0:T(8,128)}, f32[64,512]{1,0:T(8,128)}, f32[1,64]{1,0:T(1...) custom-call(bf16[1024,512]{1,0:T(8,128)(2,1)S(1)} %get-tuple-element.25.refs_0_, ...), custom_call_target="tpu_custom_call" | custom-call | tf_op jit(solution)/shard_map/pallas_call | solution.py:878

commit v6 on v4

--- a/solution.py
+++ b/solution.py
@@ -69,10 +69,10 @@
 class Copies:
     def __init__(self, send_sems, recv_sems):
         self.send_sems, self.recv_sems, self.used = send_sems, recv_sems, 0
-        self.free = list(range(send_sems.shape[0]))
+        self.free = list(range(send_sems.shape[0]))[::-1]
 
     def start(self, source, target, device):
-        slot = self.free.pop(0)
+        slot = self.free.pop()
         copy = pltpu.make_async_remote_copy(
             src_ref=source,
             dst_ref=target,
@@ -532,8 +532,8 @@
             red_ni.put(first, last, 0, d_ni, value)
             red_ni.pair(first, last)
             if first == 0:
+                node_message()
                 red_no.step1(0, zs)
-        node_message()
         red_ni.step1(0, half)
         staggered(edge_tiles, edge_stages, hooks={2: lambda: red_ni.step1(half, zs)})
         send_back()
@@ -825,7 +825,7 @@
     else:
         summed_shapes = [jax.ShapeDtypeStruct((w.shape[0], width), F32) for w in weights]
         summed_shapes += [jax.ShapeDtypeStruct((PACK, width), F32)]
-    in_flight = n_copies // 2 + 4 if fused else n_copies
+    in_flight = n_copies // 3 + 1 if fused else n_copies
     scratch += [pltpu.SemaphoreType.DMA((in_flight,)), pltpu.SemaphoreType.DMA((n_copies,))]
     scratch += reductions
 

time: 52.7 us -> 53.1 us (level)
  no operation moved by 1% of the time
where the time goes in v6:
time: 53.1 us; the launch traced here: 53 us
  Pallas kernels  51.5 us (97%)
  between operations  1.45 us (3%)
    pallas_call x1, Pallas kernels, local(): pl.pallas_call(functools.partial(kernel, sizes), out_shape=[big((edges, w...  49.8 us
    pallas_call x1, Pallas kernels, local(): pl.pallas_call(functools.partial(closing, factor, depths), out_shape=[jax...  1.69 us

profile of v6, /device:TPU:0, one launch (start us, length us, event | category | flops | bytes accessed | tf_op | source)
XLA Modules:
  0.0 53.0 jit_solution(5691475269816272350)
XLA Ops:
  1.3 49.8 %shard_map.197 = (bf16[1024,512]{1,0:T(8,128)(2,1)S(1)}, bf16[1024,512]{1,0:T(8,128)(2,1)S(1)}, bf16[4,64,128]{2,1,0:T(8,128)(2,1)S(1)}, bf16[4,128,128]{2,1,0:T...) custom-call(bf16[1024,512]{1,0:T(8,128)(2,1)} %bitcast.12, ...), custom_call_target="tpu_custom_call" | custom-call | tf_op jit(solution)/shard_map/pallas_call | solution.py:836
  51.1 1.7 %shard_map.198 = (bf16[1024,512]{1,0:T(8,128)(2,1)}, bf16[1024,512]{1,0:T(8,128)(2,1)}, f32[192,512]{1,0:T(8,128)}, f32[64,512]{1,0:T(8,128)}, f32[1,64]{1,0:T(1...) custom-call(bf16[1024,512]{1,0:T(8,128)(2,1)S(1)} %get-tuple-element.24.refs_0_, ...), custom_call_target="tpu_custom_call" | custom-call | tf_op jit(solution)/shard_map/pallas_call | solution.py:851
